TPU v7x, 128 devices: a whole 4x4x4 slice. The times are simulated.
128 devices in a mesh: gx: 8 (over x_hi, z), gy: 16 (over y, x_lo, core).
Axes of the slice: x: 4 (x_hi: 2, x_lo: 2; x = x_hi * 2 + x_lo), y: 4, z: 4, core: 2. Of those that a mesh axis runs over, the one named last changes fastest.
Arguments:
- state: float32 [10, 32, 131072], P(None, None, ('gx', 'gy'))
- kdist: bfloat16 [224, 32], replicated, may hold values from 9.9658966e-05 to 0.049804688
- rayleigh: float32 [224], replicated, may hold values from 0.002 to 0.05
- solar: float32 [224], replicated, may hold values from 0.002 to 0.01
- span_map: int32 [131072], P(('gx', 'gy')), may hold values from 0 to 131071, as said below
- cos_zenith: float32 [131072], P(('gx', 'gy')), may hold values from -1 to 1, as said below
- day_flag: int32 [131072], P(('gx', 'gy')), may hold values from 0 to 1, as said below
- albedo: float32 [131072], P(('gx', 'gy')), may hold values from 0.05 to 0.8
Outputs:
- heating: float32 [32, 131072], P(None, ('gx', 'gy'))
- surface: float32 [3, 131072], P(None, ('gx', 'gy'))
Inputs may be any that keep to these rules, and one draw needn't show every extreme that they name: span_map is a permutation of the 131072 columns; a column held by device s (index in gx+gy order) goes to a column p with (p % 1024) // 8 == s, and each device's columns reach every device equally often. `cos_zenith`: column j of device d (index in gx+gy order) and column 1023 - j of the device whose index differs from d by 64 are antipodes: their values are opposite, of magnitude 0.05 or more. `day_flag`: 1 exactly where cos_zenith > 0.
All inputs are finite; a program needn't handle non-finite values.
Results may differ from a plain program's by a relative error of at most 0.00069.
Values sent between devices are 32-bit elements; how exact they have to be, the bound alone decides.
No kernel may reach another device: no remote copies, remote signals or barrier semaphores. Data moves between devices by JAX's collectives and lax.ppermute only.
A program may use at most 64 MiB of HBM per device.

v0:
```python
import math

import jax
import jax.numpy as jnp
from jax import lax
from jax.sharding import PartitionSpec as P

diffusivity = 1.66
heat_factor = 8.0


def upward(carried, layer):
    albedo_below, source_below = carried
    reflect, transmit, direct_src = layer
    divisor = 1.0 - reflect * albedo_below
    albedo_top = reflect + transmit * transmit * albedo_below / divisor
    source_top = direct_src + transmit * (source_below + albedo_below * direct_src) / divisor
    return ((albedo_top, source_top), (albedo_below, source_below))


def downward(diffuse, layer):
    reflect, transmit, direct_src, albedo_below, source_below = layer
    lower_down = (transmit * diffuse + direct_src + reflect * source_below) / (
        1.0 - reflect * albedo_below
    )
    lower_up = albedo_below * lower_down + source_below
    return (lower_down, (lower_down, lower_up))


def column_physics(quantity_bundle, cosine, albedo, kdist, rayleigh, solar):
    levels = quantity_bundle.shape[1]
    columns = quantity_bundle.shape[2]
    kelvin_profile = quantity_bundle[0] / 250.0
    slab_weight_per_area = quantity_bundle[1]
    expansion_modes = jnp.stack(
        [
            jnp.ones_like(kelvin_profile),
            kelvin_profile,
            kelvin_profile * kelvin_profile,
            1.0 / kelvin_profile,
        ]
    )
    predictors = (quantity_bundle[2:, None] * expansion_modes[None] * slab_weight_per_area).astype(
        jnp.bfloat16
    )
    predictors = predictors.reshape(-1, levels, columns)
    block_width = math.gcd(kdist.shape[0], 32)
    blocks = kdist.shape[0] // block_width

    def one_block(block_index):
        start = block_index * block_width
        k_rows = lax.dynamic_slice_in_dim(kdist, start, block_width, 0)
        ray_rows = lax.dynamic_slice_in_dim(rayleigh, start, block_width, 0)
        sun_rows = lax.dynamic_slice_in_dim(solar, start, block_width, 0)
        tau_gas = jnp.einsum("gp,plc->lgc", k_rows, predictors, preferred_element_type=jnp.float32)
        tau_ray = ray_rows[None, :, None] * slab_weight_per_area[:, None, :]
        optical = tau_gas + tau_ray
        albedo_single = tau_ray / optical
        extinct = jnp.exp(-diffusivity * optical)
        reflect = 0.5 * albedo_single * (1.0 - extinct)
        transmit = extinct + reflect
        cumulative = jnp.cumsum(optical, axis=0)
        above = cumulative - optical
        direct_top = sun_rows[None, :, None] * cosine * jnp.exp(-above / cosine)
        direct_bottom = sun_rows[:, None] * cosine * jnp.exp(-cumulative[-1] / cosine)
        direct_src = 0.5 * albedo_single * (1.0 - jnp.exp(-optical / cosine)) * direct_top
        start_albedo = jnp.broadcast_to(albedo, direct_bottom.shape)
        (albedo_end, source_top), (albedo_below, source_below) = lax.scan(
            upward,
            (start_albedo, albedo * direct_bottom),
            (reflect, transmit, direct_src),
            reverse=True,
            unroll=True,
        )
        zeros = jnp.zeros_like(direct_bottom)
        final_down, (lower_down, lower_up) = lax.scan(
            downward,
            zeros,
            (reflect, transmit, direct_src, albedo_below, source_below),
            unroll=True,
        )
        direct_all = jnp.concatenate([direct_top, direct_bottom[None]], 0)
        down_all = jnp.concatenate([zeros[None], lower_down], 0)
        up_all = jnp.concatenate([source_top[None], lower_up], 0)
        net = jnp.sum(direct_all + down_all - up_all, axis=1)
        surface = jnp.stack(
            [jnp.sum(direct_bottom, 0), jnp.sum(final_down, 0), jnp.sum(source_top, 0)]
        )
        return (net, surface)

    nets, surfaces = lax.map(one_block, jnp.arange(blocks, dtype=jnp.int32))
    net = jnp.sum(nets, 0)
    heat_rate = heat_factor * (net[:-1] - net[1:]) / slab_weight_per_area
    return (heat_rate, jnp.sum(surfaces, 0))


def local(state, kdist, rayleigh, solar, span_map, cos_zenith, day_flag, albedo):
    columns = state.shape[-1]
    devices = lax.axis_size(("gx", "gy"))
    per_peer = columns // devices
    slot_index = span_map // columns * per_peer + span_map % per_peer
    daylit = day_flag.astype(jnp.float32)
    outgoing = jnp.zeros_like(state).at[:, :, slot_index].set(state)
    quantity_bundle = lax.all_to_all(
        outgoing, ("gx", "gy"), split_axis=2, concat_axis=2, tiled=True
    )
    cosine = jnp.where(day_flag == 1, cos_zenith, jnp.float32(1.0))
    heat_rate, surface = column_physics(quantity_bundle, cosine, albedo, kdist, rayleigh, solar)
    heat_rate = heat_rate * daylit
    surface = surface * daylit
    returned = lax.all_to_all(heat_rate, ("gx", "gy"), split_axis=1, concat_axis=1, tiled=True)
    heating = jnp.take(returned, slot_index, axis=1)
    return (heating, surface)


def solution(mesh):
    in_specs = (
        P(None, None, ("gx", "gy")),
        P(),
        P(),
        P(),
        P(("gx", "gy")),
        P(("gx", "gy")),
        P(("gx", "gy")),
        P(("gx", "gy")),
    )
    out_specs = (P(None, ("gx", "gy")), P(None, ("gx", "gy")))
    return jax.shard_map(local, mesh=mesh, in_specs=in_specs, out_specs=out_specs, check_vma=False)
```

profile of v0, /device:TPU:1, one launch (start us, length us, event | category | flops | bytes accessed | tf_op | source)
XLA Modules:
  0.0 615.0 jit_solution(5570828384727879722)
XLA Ops:
  1.9 7.1 %copy.44 = f32[1024,10,32]{2,1,0:T(8,128)} copy(f32[1024,10,32]{0,2,1:T(8,128)} %bitcast.1235) | data formatting | bytes 2621440 | tf_op args[0]
  9.0 3.9 broadcast_in_dim.249
  12.8 118.0 %scatter_fusion = f32[10,32,1024]{1,0,2:T(8,128)} fusion(f32[10,32,1024]{1,0,2:T(8,128)} %broadcast_in_dim.249, s32[1024]{0:T(1024)S(1)} %get-tuple-element.294, f32[1024,10,32]{2,1,0:T(8,128)} %copy.44), kind=kCustom, calls=%fused_computation.1 | custom fusion | bytes 3936256 | tf_op jit(solution)/shard_map/scatter | solution.py:103
  130.8 7.1 %reshape.118 = f32[128,1,2560]{2,1,0:T(1,128)} reshape(f32[1024,10,32]{2,1,0:T(8,128)} %bitcast.1229) | data formatting | bytes 2621440
  137.9 11.4 %all-to-all-start = ((f32[128,1,2560]{2,1,0:T(1,128)}), f32[128,1,2560]{2,1,0:T(1,128)S(1)}, u32[]{:S(2)}, u32[]{:S(2)}) async-start(f32[128,1,2560]{2,1,0:T(1,128)} %reshape.118), calls=%async_computation | async-start | bytes 2621440 | tf_op jit(solution)/shard_map/all_to_all | solution.py:104
  150.5 20.5 %all-to-all-done = f32[128,1,2560]{2,1,0:T(1,128)S(1)} async-done(((f32[128,1,2560]{2,1,0:T(1,128)}), f32[128,1,2560]{2,1,0:T(1,128)S(1)}, u32[]{:S(2)}, u32[]{:S(2)}) %all-to-all-start) | async-done | bytes 1310752 | tf_op jit(solution)/shard_map/all_to_all | solution.py:104
  175.3 4.7 reshape.119
  180.1 4.2 fusion.25
  184.3 5.9 slice.605
  194.4 396.4 %while.13 = (s32[]{:T(128)}, f32[7,33,1024]{2,1,0:T(8,128)}, f32[7,3,1024]{2,1,0:T(4,128)}, s32[7]{0:T(128)S(1)}, f32[224]{0:T(256)S(1)}, /*index=5*/f32[1024]{0...) while((s32[]{:T(128)}, f32[7,33,1024]{2,1,0:T(8,128)}, ...), condition=%wide.region_7.8_spmd.clone, body=%wide.region_1.7_spmd.clone.sunk | while | flops 147589120 | bytes 160038896 | solution.py:91
  200.0 5.4 mul.2185
  208.4 22.8 %fusion.39 = f32[32,32,1024]{2,1,0:T(8,128)S(1)} fusion(f32[32,32,1024]{2,1,0:T(8,128)S(1)} %multiply_add_fusion.2), kind=kOutput, calls=%fused_computation.350.clone.1 | output fusion | flops 32505856 | bytes 8388608 | tf_op jit(solution)/shard_map/while/body/eval_jaxpr/jit(cumsum)/reduce_window_sum | solution.py:62
  236.1 3.8 fusion.42
  256.6 5.4 mul.2185
  265.0 22.8 %fusion.39 = f32[32,32,1024]{2,1,0:T(8,128)S(1)} fusion(f32[32,32,1024]{2,1,0:T(8,128)S(1)} %multiply_add_fusion.2), kind=kOutput, calls=%fused_computation.350.clone.1 | output fusion | flops 32505856 | bytes 8388608 | tf_op jit(solution)/shard_map/while/body/eval_jaxpr/jit(cumsum)/reduce_window_sum | solution.py:62
  292.8 3.8 fusion.42
  313.2 5.4 mul.2185
  321.6 22.8 %fusion.39 = f32[32,32,1024]{2,1,0:T(8,128)S(1)} fusion(f32[32,32,1024]{2,1,0:T(8,128)S(1)} %multiply_add_fusion.2), kind=kOutput, calls=%fused_computation.350.clone.1 | output fusion | flops 32505856 | bytes 8388608 | tf_op jit(solution)/shard_map/while/body/eval_jaxpr/jit(cumsum)/reduce_window_sum | solution.py:62
  349.4 3.8 fusion.42
  369.8 5.4 mul.2185
  378.2 22.8 %fusion.39 = f32[32,32,1024]{2,1,0:T(8,128)S(1)} fusion(f32[32,32,1024]{2,1,0:T(8,128)S(1)} %multiply_add_fusion.2), kind=kOutput, calls=%fused_computation.350.clone.1 | output fusion | flops 32505856 | bytes 8388608 | tf_op jit(solution)/shard_map/while/body/eval_jaxpr/jit(cumsum)/reduce_window_sum | solution.py:62
  406.0 3.8 fusion.42
  426.4 5.4 mul.2185
  434.8 22.8 %fusion.39 = f32[32,32,1024]{2,1,0:T(8,128)S(1)} fusion(f32[32,32,1024]{2,1,0:T(8,128)S(1)} %multiply_add_fusion.2), kind=kOutput, calls=%fused_computation.350.clone.1 | output fusion | flops 32505856 | bytes 8388608 | tf_op jit(solution)/shard_map/while/body/eval_jaxpr/jit(cumsum)/reduce_window_sum | solution.py:62
  462.6 3.8 fusion.42
  483.0 5.4 mul.2185
  491.4 22.8 %fusion.39 = f32[32,32,1024]{2,1,0:T(8,128)S(1)} fusion(f32[32,32,1024]{2,1,0:T(8,128)S(1)} %multiply_add_fusion.2), kind=kOutput, calls=%fused_computation.350.clone.1 | output fusion | flops 32505856 | bytes 8388608 | tf_op jit(solution)/shard_map/while/body/eval_jaxpr/jit(cumsum)/reduce_window_sum | solution.py:62
  519.2 3.8 fusion.42
  539.6 5.4 mul.2185
  548.0 22.8 %fusion.39 = f32[32,32,1024]{2,1,0:T(8,128)S(1)} fusion(f32[32,32,1024]{2,1,0:T(8,128)S(1)} %multiply_add_fusion.2), kind=kOutput, calls=%fused_computation.350.clone.1 | output fusion | flops 32505856 | bytes 8388608 | tf_op jit(solution)/shard_map/while/body/eval_jaxpr/jit(cumsum)/reduce_window_sum | solution.py:62
  595.0 5.0 all-to-all-start.1
  600.6 9.4 %all-to-all-done.1 = f32[128,1,256]{2,1,0:T(1,128)S(1)} async-done(((f32[128,1,256]{2,1,0:T(1,128)}), f32[128,1,256]{2,1,0:T(1,128)S(1)}, u32[]{:S(2)}, u32[]{:S(2)}) %all-to-all-start.1) | async-done | bytes 131104 | tf_op jit(solution)/shard_map/all_to_all | solution.py:111
  (1010 shorter events, 187.5 us)
Async XLA Ops:
  130.8 18.5 %copy-start.47 = (s32[1024]{0:T(1024)S(1)}, s32[1024]{0:T(1024)}, u32[]{:S(2)}) copy-start(s32[1024]{0:T(1024)} %param.16) | copy-start | bytes 12292
  130.8 19.7 %copy-start.49 = (f32[1024]{0:T(1024)S(1)}, f32[1024]{0:T(1024)}, u32[]{:S(2)}) copy-start(f32[1024]{0:T(1024)} %param.15) | copy-start | bytes 12292
  137.9 33.2 %all-to-all-start = ((f32[128,1,2560]{2,1,0:T(1,128)}), f32[128,1,2560]{2,1,0:T(1,128)S(1)}, u32[]{:S(2)}, u32[]{:S(2)}) async-start(f32[128,1,2560]{2,1,0:T(1,128)} %reshape.118), calls=%async_computation | async-start | bytes 2621440 | tf_op jit(solution)/shard_map/all_to_all | solution.py:104
  194.6 10.7 %copy-start.4 = (f32[4,32,1024]{2,0,1:T(4,128)}, f32[4,32,1024]{2,0,1:T(4,128)S(1)}, u32[]{:S(2)}) copy-start(f32[4,32,1024]{2,0,1:T(4,128)S(1)} %get-tuple-element.836) | copy-start | bytes 1572868 | tf_op jit(solution)/shard_map/while
  240.1 7.0 %copy-start.29 = (f32[32,1024]{1,0:T(8,128)S(1)}, f32[32,1024]{1,0:T(8,128)}, u32[]{:S(2)}) copy-start(f32[32,1024]{1,0:T(8,128)} %get-tuple-element.718) | copy-start | bytes 393220 | tf_op jit(solution)/shard_map/while
  240.1 7.0 %copy-start.30 = (f32[32,1024]{1,0:T(8,128)S(1)}, f32[32,1024]{1,0:T(8,128)}, u32[]{:S(2)}) copy-start(f32[32,1024]{1,0:T(8,128)} %get-tuple-element.720) | copy-start | bytes 393220 | tf_op jit(solution)/shard_map/while
  251.2 10.7 %copy-start.4 = (f32[4,32,1024]{2,0,1:T(4,128)}, f32[4,32,1024]{2,0,1:T(4,128)S(1)}, u32[]{:S(2)}) copy-start(f32[4,32,1024]{2,0,1:T(4,128)S(1)} %get-tuple-element.836) | copy-start | bytes 1572868 | tf_op jit(solution)/shard_map/while
  296.7 7.1 %copy-start.29 = (f32[32,1024]{1,0:T(8,128)S(1)}, f32[32,1024]{1,0:T(8,128)}, u32[]{:S(2)}) copy-start(f32[32,1024]{1,0:T(8,128)} %get-tuple-element.718) | copy-start | bytes 393220 | tf_op jit(solution)/shard_map/while
  296.7 7.1 %copy-start.30 = (f32[32,1024]{1,0:T(8,128)S(1)}, f32[32,1024]{1,0:T(8,128)}, u32[]{:S(2)}) copy-start(f32[32,1024]{1,0:T(8,128)} %get-tuple-element.720) | copy-start | bytes 393220 | tf_op jit(solution)/shard_map/while
  296.8 7.0 %copy-start.27 = (f32[32,1024]{1,0:T(8,128)S(1)}, f32[32,1024]{1,0:T(8,128)}, u32[]{:S(2)}) copy-start(f32[32,1024]{1,0:T(8,128)} %get-tuple-element.722) | copy-start | bytes 393220 | tf_op jit(solution)/shard_map/while
  296.8 7.0 %copy-start.28 = (f32[32,1024]{1,0:T(8,128)S(1)}, f32[32,1024]{1,0:T(8,128)}, u32[]{:S(2)}) copy-start(f32[32,1024]{1,0:T(8,128)} %get-tuple-element.724) | copy-start | bytes 393220 | tf_op jit(solution)/shard_map/while
  307.8 10.7 %copy-start.4 = (f32[4,32,1024]{2,0,1:T(4,128)}, f32[4,32,1024]{2,0,1:T(4,128)S(1)}, u32[]{:S(2)}) copy-start(f32[4,32,1024]{2,0,1:T(4,128)S(1)} %get-tuple-element.836) | copy-start | bytes 1572868 | tf_op jit(solution)/shard_map/while
  353.3 7.0 %copy-start.29 = (f32[32,1024]{1,0:T(8,128)S(1)}, f32[32,1024]{1,0:T(8,128)}, u32[]{:S(2)}) copy-start(f32[32,1024]{1,0:T(8,128)} %get-tuple-element.718) | copy-start | bytes 393220 | tf_op jit(solution)/shard_map/while
  353.3 7.0 %copy-start.30 = (f32[32,1024]{1,0:T(8,128)S(1)}, f32[32,1024]{1,0:T(8,128)}, u32[]{:S(2)}) copy-start(f32[32,1024]{1,0:T(8,128)} %get-tuple-element.720) | copy-start | bytes 393220 | tf_op jit(solution)/shard_map/while
  364.4 10.7 %copy-start.4 = (f32[4,32,1024]{2,0,1:T(4,128)}, f32[4,32,1024]{2,0,1:T(4,128)S(1)}, u32[]{:S(2)}) copy-start(f32[4,32,1024]{2,0,1:T(4,128)S(1)} %get-tuple-element.836) | copy-start | bytes 1572868 | tf_op jit(solution)/shard_map/while
  409.9 7.0 %copy-start.29 = (f32[32,1024]{1,0:T(8,128)S(1)}, f32[32,1024]{1,0:T(8,128)}, u32[]{:S(2)}) copy-start(f32[32,1024]{1,0:T(8,128)} %get-tuple-element.718) | copy-start | bytes 393220 | tf_op jit(solution)/shard_map/while
  409.9 7.0 %copy-start.30 = (f32[32,1024]{1,0:T(8,128)S(1)}, f32[32,1024]{1,0:T(8,128)}, u32[]{:S(2)}) copy-start(f32[32,1024]{1,0:T(8,128)} %get-tuple-element.720) | copy-start | bytes 393220 | tf_op jit(solution)/shard_map/while
  421.0 10.7 %copy-start.4 = (f32[4,32,1024]{2,0,1:T(4,128)}, f32[4,32,1024]{2,0,1:T(4,128)S(1)}, u32[]{:S(2)}) copy-start(f32[4,32,1024]{2,0,1:T(4,128)S(1)} %get-tuple-element.836) | copy-start | bytes 1572868 | tf_op jit(solution)/shard_map/while
  466.5 7.1 %copy-start.29 = (f32[32,1024]{1,0:T(8,128)S(1)}, f32[32,1024]{1,0:T(8,128)}, u32[]{:S(2)}) copy-start(f32[32,1024]{1,0:T(8,128)} %get-tuple-element.718) | copy-start | bytes 393220 | tf_op jit(solution)/shard_map/while
  466.5 7.1 %copy-start.30 = (f32[32,1024]{1,0:T(8,128)S(1)}, f32[32,1024]{1,0:T(8,128)}, u32[]{:S(2)}) copy-start(f32[32,1024]{1,0:T(8,128)} %get-tuple-element.720) | copy-start | bytes 393220 | tf_op jit(solution)/shard_map/while
  466.6 7.0 %copy-start.27 = (f32[32,1024]{1,0:T(8,128)S(1)}, f32[32,1024]{1,0:T(8,128)}, u32[]{:S(2)}) copy-start(f32[32,1024]{1,0:T(8,128)} %get-tuple-element.722) | copy-start | bytes 393220 | tf_op jit(solution)/shard_map/while
  466.6 7.0 %copy-start.28 = (f32[32,1024]{1,0:T(8,128)S(1)}, f32[32,1024]{1,0:T(8,128)}, u32[]{:S(2)}) copy-start(f32[32,1024]{1,0:T(8,128)} %get-tuple-element.724) | copy-start | bytes 393220 | tf_op jit(solution)/shard_map/while
  477.6 10.7 %copy-start.4 = (f32[4,32,1024]{2,0,1:T(4,128)}, f32[4,32,1024]{2,0,1:T(4,128)S(1)}, u32[]{:S(2)}) copy-start(f32[4,32,1024]{2,0,1:T(4,128)S(1)} %get-tuple-element.836) | copy-start | bytes 1572868 | tf_op jit(solution)/shard_map/while
  523.1 7.0 %copy-start.29 = (f32[32,1024]{1,0:T(8,128)S(1)}, f32[32,1024]{1,0:T(8,128)}, u32[]{:S(2)}) copy-start(f32[32,1024]{1,0:T(8,128)} %get-tuple-element.718) | copy-start | bytes 393220 | tf_op jit(solution)/shard_map/while
  523.1 7.0 %copy-start.30 = (f32[32,1024]{1,0:T(8,128)S(1)}, f32[32,1024]{1,0:T(8,128)}, u32[]{:S(2)}) copy-start(f32[32,1024]{1,0:T(8,128)} %get-tuple-element.720) | copy-start | bytes 393220 | tf_op jit(solution)/shard_map/while
  534.2 10.7 %copy-start.4 = (f32[4,32,1024]{2,0,1:T(4,128)}, f32[4,32,1024]{2,0,1:T(4,128)S(1)}, u32[]{:S(2)}) copy-start(f32[4,32,1024]{2,0,1:T(4,128)S(1)} %get-tuple-element.836) | copy-start | bytes 1572868 | tf_op jit(solution)/shard_map/while
  579.7 7.0 %copy-start.29 = (f32[32,1024]{1,0:T(8,128)S(1)}, f32[32,1024]{1,0:T(8,128)}, u32[]{:S(2)}) copy-start(f32[32,1024]{1,0:T(8,128)} %get-tuple-element.718) | copy-start | bytes 393220 | tf_op jit(solution)/shard_map/while
  579.7 7.0 %copy-start.30 = (f32[32,1024]{1,0:T(8,128)S(1)}, f32[32,1024]{1,0:T(8,128)}, u32[]{:S(2)}) copy-start(f32[32,1024]{1,0:T(8,128)} %get-tuple-element.720) | copy-start | bytes 393220 | tf_op jit(solution)/shard_map/while
  590.8 9.2 %copy-start.45 = (f32[1024]{0:T(1024)S(1)}, f32[1024]{0:T(1024)}, u32[]{:S(2)}) copy-start(f32[1024]{0:T(1024)} %convert_element_type.8) | copy-start | bytes 12292
  590.8 20.3 %copy-start.46 = (s32[1024]{0:T(1024)S(1)}, s32[1024]{0:T(1024)}, u32[]{:S(2)}) copy-start(s32[1024]{0:T(1024)} %broadcast_clamp_fusion) | copy-start | bytes 12292
  590.8 23.1 %copy-start.48 = (pred[1024]{0:T(1024)(128)(4,1)S(1)}, pred[1024]{0:T(1024)(128)(4,1)}, u32[]{:S(2)}) copy-start(pred[1024]{0:T(1024)(128)(4,1)} %get-tuple-element.293) | copy-start | bytes 3076
  595.0 15.0 %all-to-all-start.1 = ((f32[128,1,256]{2,1,0:T(1,128)}), f32[128,1,256]{2,1,0:T(1,128)S(1)}, u32[]{:S(2)}, u32[]{:S(2)}) async-start(f32[128,1,256]{2,1,0:T(1,128)} %reshape.120), calls=%async_computation.1 | async-start | bytes 262144 | tf_op jit(solution)/shard_map/all_to_all | solution.py:111
  (299 other events, 1102.1 us)
where the time goes:
time: 619 us; the launch traced here: 615 us
  other arithmetic  315 us (51%)
  local copies, waits for them, and re-layouts  222 us (36%)
  waiting for transfers between devices  29.9 us (5%)
  matrix products  21.2 us (3%)
  starting transfers between devices  16.4 us (3%)
  loops' own time  9.77 us (2%)
    another operation x7, other arithmetic, one_block(): cumulative = jnp.cumsum(optical, axis=0)  160 us
    scatter x1, local copies, waits for them, and re-layouts, local(): outgoing = jnp.zeros_like(state).at[:, :, slot_index].set(state)  118 us
    while x217, other arithmetic  43.2 us
    mul x7, local copies, waits for them, and re-layouts, column_physics(): quantity_bundle[2:, None] * expansion_modes[None] * slab_weight_per_area  37.5 us
    reduce_sum x7, other arithmetic, one_block(): jnp.sum(final_down, 0)  26.7 us
    unnamed x25, local copies, waits for them, and re-layouts  24.9 us
    add x7, other arithmetic, one_block(): transmit = extinct + reflect  23.6 us
    mul x7, other arithmetic, column_physics(): quantity_bundle[2:, None] * expansion_modes[None] * slab_weight_per_area  22.3 us
  transfers between devices with their start and end apart: 2, of which 2 were waited for; matrix products, arithmetic and copies ran while one was open for 0% of the time, Pallas kernels for 0%

commit v1 on v0

v1 whole, which is shorter than its diff:
```python
import jax
import jax.numpy as jnp
from jax import lax
from jax.experimental import pallas as pl
from jax.experimental.pallas import tpu as pltpu
from jax.sharding import PartitionSpec as P

AXES = ("gx", "gy")
F32 = jnp.float32
BF16 = jnp.bfloat16
LOG2E = 1.4426950408889634
DIFFUSIVITY = 1.66
HEAT_FACTOR = 8.0
LANES = 128
HALF = 64
CHUNK = 256


def split3(x):
    hi = x.astype(BF16)
    rest = x - hi.astype(F32)
    mid = rest.astype(BF16)
    low = (rest - mid.astype(F32)).astype(BF16)
    return hi, mid, low


def dot(a, b, dims=((1,), (0,))):
    return lax.dot_general(a, b, (dims, ((), ())), preferred_element_type=F32)


def iota(shape, dim):
    return lax.broadcasted_iota(jnp.int32, shape, dim)


def send_kernel(cos_ref, day_ref, alb_ref, out_ref):
    rows = cos_ref.shape[0]
    devices = out_ref.shape[0]
    group = devices // rows
    per = LANES // group
    keep = iota((devices, LANES), 1) // per == iota((devices, LANES), 0) % group
    cosine = jnp.where(day_ref[...] == 1, cos_ref[...], 0.0)

    def spread(x):
        x = jnp.broadcast_to(x[:, None, :], (rows, group, LANES)).reshape(devices, LANES)
        return jnp.where(keep, x, 0.0)

    out_ref[...] = spread(cosine) + pltpu.roll(spread(alb_ref[...]), per, 1)


def main_kernel(
    shift_ref,
    state_ref,
    recv_ref,
    span_ref,
    lhs_ref,
    rayh_ref,
    sun_ref,
    heat_ref,
    send_ref,
    pred_s,
    gather_s,
    pick_s,
    tau_s,
    trans_s,
    emit_s,
    back_s,
    net_s,
    sfc_s,
    mass_s,
    out_s,
    fin_s,
):
    levels, columns = state_ref.shape[1:]
    gases = state_ref.shape[0] - 2
    npred = 4 * gases
    devices = recv_ref.shape[0]
    per = columns // devices
    grows = rayh_ref.shape[0]
    base = npred * levels
    tail = base + 3 * levels
    gtail = base + 8 * levels

    t = state_ref[0] / 250.0
    m = state_ref[1]
    modes = (None, t, t * t, 1.0 / t)
    for i in range(gases):
        q = state_ref[2 + i]
        for b in range(4):
            v = (q if b == 0 else q * modes[b]) * m
            pred_s[pl.ds((4 * i + b) * levels, levels), :] = v.astype(BF16)
    for j, term in enumerate(split3(m)):
        pred_s[pl.ds(base + j * levels, levels), :] = term

    span = span_ref[...]

    def owner_hot():
        return jnp.where(iota((devices, columns), 0) == span // columns, 1.0, 0.0).astype(BF16)

    slot_hot = iota((per, columns), 0) == span % per
    recv = pltpu.roll(recv_ref[...], shift_ref[0], 1).T[: 2 * per]
    sel = dot(jnp.concatenate(split3(recv), 0), owner_hot())
    sel = sel[: 2 * per] + sel[2 * per : 4 * per] + sel[4 * per :]
    cos_e = jnp.sum(jnp.where(slot_hot, sel[:per], 0.0), 0, keepdims=True)
    alb_e = jnp.sum(jnp.where(slot_hot, sel[per:], 0.0), 0, keepdims=True)
    extra = [x.astype(F32) for x in (*split3(cos_e), *split3(alb_e))]
    extra = jnp.concatenate(extra + [jnp.zeros((10, columns), F32)], 0)
    pred_s[pl.ds(tail, 16), :] = extra.astype(BF16)

    day = jnp.where(cos_e > 0.0, 1.0, 0.0)
    rows = columns // LANES
    day2 = jnp.concatenate([day[:, r * LANES : (r + 1) * LANES] for r in range(rows)], 0)
    upper = jnp.where(iota((LANES, LANES), 0) <= iota((LANES, LANES), 1), 1.0, 0.0)
    within = dot(day2.astype(BF16), upper.astype(BF16))
    place = []
    offset = jnp.zeros((1, 1), F32)
    for r in range(rows):
        place.append(within[r : r + 1] + offset)
        offset = offset + within[r : r + 1, LANES - 1 :]
    order = jnp.where(day > 0.0, jnp.concatenate(place, 1) - 1.0, -1.0).astype(jnp.int32)
    count = jnp.sum(day).astype(jnp.int32)
    chunks = (count + CHUNK - 1) // CHUNK
    blocks = (count + HALF - 1) // HALF

    out_s[...] = jnp.zeros_like(out_s)
    fin_s[...] = jnp.zeros_like(fin_s)

    def gather(c, _):
        start = pl.multiple_of(c * CHUNK, CHUNK)
        hot = jnp.where(iota((CHUNK, columns), 0) + start == order, 1.0, 0.0).astype(BF16)
        pick_s[pl.ds(start, CHUNK), :] = hot
        out = dot(pred_s[...], hot, ((1,), (1,)))
        for j in range(CHUNK // LANES):
            piece = out[:, j * LANES : (j + 1) * LANES]
            at = c * (CHUNK // LANES) + j
            gather_s[at, pl.ds(0, base), :] = piece[:base]
            for r, k in enumerate((0, 0, 0, 1, 1, 2)):
                gather_s[at, pl.ds(base + r * levels, levels), :] = piece[
                    base + k * levels : base + (k + 1) * levels
                ]
            gather_s[at, pl.ds(base + 6 * levels, 2 * levels), :] = jnp.zeros(
                (2 * levels, LANES), F32
            )
            gather_s[at, pl.ds(gtail, 8), :] = piece[tail : tail + 8]
        return 0

    lax.fori_loop(0, chunks, gather, 0)

    lane_low = iota((1, LANES), 1) < HALF
    part = grows // 2

    def fold(x):
        return jnp.sum(x.reshape(x.shape[0] // 8, 8, LANES), 0)

    def block(b, _):
        chunk = b // 2
        odd = b % 2
        shift = HALF * odd

        def duplicate(x):
            return jnp.where(
                lane_low, pltpu.roll(x, shift, 1), pltpu.roll(x, HALF - shift, 1)
            )

        def tau_level(l, _):
            x = duplicate(gather_s[chunk, pl.ds(l, npred + 8, stride=levels), :])
            x = jnp.concatenate([jnp.where(lane_low, x, 0.0), jnp.where(lane_low, 0.0, x)], 0)
            tau_s[l] = dot(lhs_ref[...], x.astype(BF16))
            return 0

        lax.fori_loop(0, levels, tau_level, 0, unroll=4)

        ex = duplicate(gather_s[chunk, pl.ds(gtail, 8), :])
        cosine = ex[0:1] + ex[1:2] + ex[2:3]
        albedo = ex[3:4] + ex[4:5] + ex[5:6]
        slope = -LOG2E / cosine
        mass = duplicate(
            gather_s[chunk, pl.ds(base, levels), :]
            + gather_s[chunk, pl.ds(base + 3 * levels, levels), :]
            + gather_s[chunk, pl.ds(base + 5 * levels, levels), :]
        )
        mass_s[...] = mass
        net_s[...] = jnp.zeros_like(net_s)

        def group_of(gi, _):
            gs = pl.ds(pl.multiple_of(gi * part, 8), part)

            def down(l, carry):
                back, emit, direct = carry
                net_s[l] += fold(direct + emit)
                tau = tau_s[l, gs, :]
                ext = jnp.exp2(tau * (-DIFFUSIVITY * LOG2E))
                beam = jnp.exp2(tau * slope)
                half_w = rayh_ref[gs, :] * mass_s[pl.ds(l, 1), :] * pl.reciprocal(tau)
                reflect = half_w * (1.0 - ext)
                transmit = ext + reflect
                lower = direct * beam
                source = half_w * (direct - lower)
                inv = pl.reciprocal(1.0 - reflect * back)
                trans = transmit * inv
                trans_s[l, gs, :] = trans
                emit_s[l, gs, :] = (source + reflect * emit) * inv
                back_s[l, gs, :] = back
                new_back = reflect + (transmit * back) * trans
                new_emit = source + trans * (emit + back * source)
                return new_back, new_emit, lower

            zero = jnp.zeros((part, LANES), F32)
            back, emit, direct = lax.fori_loop(
                0, levels, down, (zero, zero, sun_ref[gs, :] * cosine), unroll=2
            )
            up = albedo * (emit + direct) * pl.reciprocal(1.0 - albedo * back)
            dif = emit + back * up
            sfc_s[gi, 0] = fold(direct)
            sfc_s[gi, 1] = fold(dif)
            net_s[levels] += fold(direct + dif - up)

            def rise(j, up):
                l = levels - 1 - j
                up = trans_s[l, gs, :] * up + emit_s[l, gs, :]
                net_s[l] -= fold(up - back_s[l, gs, :] * up)
                return up

            up = lax.fori_loop(0, levels, rise, up, unroll=2)
            sfc_s[gi, 2] = fold(up)
            return 0

        lax.fori_loop(0, 2, group_of, 0)

        net = jnp.sum(net_s[...], 1)
        heat = HEAT_FACTOR * (net[:levels] - net[1:])
        sfc = jnp.sum(sfc_s[0] + sfc_s[1], 1)
        out = jnp.concatenate([heat, sfc, jnp.zeros((5, LANES), F32)], 0)
        out = out + pltpu.roll(out, HALF, 1)
        out = out / jnp.concatenate([mass, jnp.ones((8, LANES), F32)], 0)
        valid = iota((1, LANES), 1) % HALF + b * HALF < count
        mine = iota((1, LANES), 1) // HALF == odd
        out_s[chunk] = jnp.where(mine, jnp.where(valid, out, 0.0), out_s[chunk])
        return 0

    lax.fori_loop(0, blocks, block, 0)

    def spread(c, _):
        two = jnp.concatenate([out_s[(CHUNK // LANES) * c + j] for j in range(CHUNK // LANES)], 1)
        rows = two.shape[0]
        back = dot(
            jnp.concatenate([x.astype(F32) for x in split3(two)], 0).astype(BF16),
            pick_s[pl.ds(pl.multiple_of(c * CHUNK, CHUNK), CHUNK), :],
        )
        fin_s[...] += back[:rows] + back[rows : 2 * rows] + back[2 * rows :]
        return 0

    lax.fori_loop(0, chunks, spread, 0)

    heat_ref[...] = fin_s[pl.ds(0, levels), :]
    sfc = fin_s[pl.ds(levels, 8), :]
    vals = jnp.concatenate([jnp.where(slot_hot, sfc[q : q + 1], 0.0) for q in range(3)], 0)
    hot = owner_hot()
    send = sum(dot(hot, x, ((1,), (1,))) for x in split3(vals))
    send_ref[...] = jnp.concatenate([send, jnp.zeros((devices, LANES - 3 * per), F32)], 1)


def recv_kernel(recv_ref, out_ref):
    devices = recv_ref.shape[0]
    width = out_ref.shape[1]
    per = width // devices
    group = LANES // per
    lane = iota((LANES, 3 * LANES), 1)
    hot = jnp.where(iota((LANES, 3 * LANES), 0) == lane // LANES * per + lane % per, 1.0, 0.0)
    hot = hot.astype(BF16)
    x = sum(dot(term, hot) for term in split3(recv_ref[...]))
    shape = (devices, 3 * LANES)
    x = jnp.where(iota(shape, 1) % LANES // per == iota(shape, 0) % group, x, 0.0)
    x = jnp.sum(x.reshape(devices // group, group, 3 * LANES), 1)
    for q in range(3):
        for r in range(devices // group):
            out_ref[q : q + 1, r * LANES : (r + 1) * LANES] = x[
                r : r + 1, q * LANES : (q + 1) * LANES
            ]


def exchange(x):
    rows = x.shape[0]
    y = lax.all_to_all(
        x.reshape(rows, 1, LANES), AXES, split_axis=0, concat_axis=0, tiled=True
    )
    return y.reshape(rows, LANES)


def local(state, kdist, rayleigh, solar, span_map, cos_zenith, day_flag, albedo):
    fields, levels, columns = state.shape
    devices = lax.axis_size(AXES)
    per = columns // devices
    group = LANES // per
    rows = columns // LANES
    npred = kdist.shape[1]
    grows = kdist.shape[0] // 2

    sent = pl.pallas_call(
        send_kernel,
        out_shape=jax.ShapeDtypeStruct((devices, LANES), F32),
        name="send",
    )(
        cos_zenith.reshape(rows, LANES),
        day_flag.reshape(rows, LANES),
        albedo.reshape(rows, LANES),
    )
    recv = exchange(sent)

    r1, r2, r3 = (x[:, None] for x in split3(rayleigh))
    zero = jnp.zeros_like(r1)
    terms = jnp.concatenate([kdist, r1, r2, r3, r1, r2, r1, zero, zero], 1)
    lhs = jnp.concatenate([terms[:grows], terms[grows:]], 1)

    def halves(x):
        return jnp.where(
            jnp.arange(LANES)[None, :] < HALF, x[:grows, None], x[grows:, None]
        )

    shift = (LANES - lax.axis_index(AXES) % group * per) % LANES
    chunks = columns // LANES
    g_array = pltpu.VMEM((levels, grows, LANES), F32)
    vmem = pl.BlockSpec(memory_space=pltpu.VMEM)
    heating, back = pl.pallas_call(
        main_kernel,
        out_shape=(
            jax.ShapeDtypeStruct((levels, columns), F32),
            jax.ShapeDtypeStruct((devices, LANES), F32),
        ),
        in_specs=[pl.BlockSpec(memory_space=pltpu.SMEM)] + [vmem] * 6,
        out_specs=(vmem, vmem),
        scratch_shapes=[
            pltpu.VMEM(((npred + 3) * levels + 16, columns), BF16),
            pltpu.VMEM((chunks, (npred + 8) * levels + 8, LANES), F32),
            pltpu.VMEM((columns, columns), BF16),
            g_array,
            g_array,
            g_array,
            g_array,
            pltpu.VMEM((levels + 1, 8, LANES), F32),
            pltpu.VMEM((2, 3, 8, LANES), F32),
            pltpu.VMEM((levels, LANES), F32),
            pltpu.VMEM((chunks, levels + 8, LANES), F32),
            pltpu.VMEM((levels + 8, columns), F32),
        ],
        compiler_params=pltpu.CompilerParams(vmem_limit_bytes=48 << 20),
        name="physics",
    )(
        shift.reshape(1).astype(jnp.int32),
        state,
        recv,
        span_map.reshape(1, columns),
        lhs,
        halves(0.5 * rayleigh),
        halves(solar),
    )
    surface = pl.pallas_call(
        recv_kernel,
        out_shape=jax.ShapeDtypeStruct((3, columns), F32),
        name="receive",
    )(exchange(back))
    return heating, surface


def solution(mesh):
    cols = P(AXES)
    in_specs = (P(None, None, AXES), P(), P(), P(), cols, cols, cols, cols)
    out_specs = (P(None, AXES), P(None, AXES))
    return jax.shard_map(
        local, mesh=mesh, in_specs=in_specs, out_specs=out_specs, check_vma=False
    )
```

time: 619 us -> 95.2 us (0.15)
  other arithmetic: 315 us -> 0.98 us
  local copies, waits for them, and re-layouts: 222 us -> 3.9 us
  Pallas kernels: 0 us -> 57.1 us
  waiting for transfers between devices: 29.9 us -> 6.57 us
  matrix products: 21.2 us -> 0 us
  blocking collectives: 0 us -> 14.1 us
  loops' own time: 9.77 us -> 0 us
    another operation x8 -> x0, other arithmetic: 160 us -> none  [the longest x7 160 us: one_block(): cumulative = jnp.cumsum(optical, axis=0)]
    scatter x1 -> x0, local copies, waits for them, and re-layouts: 118 us -> none  [local(): outgoing = jnp.zeros_like(state).at[:, :, slot_index].set(state)]
    pallas_call x0 -> x3, Pallas kernels: none -> 57.1 us  [the longest x1 53.9 us: local(): pl.pallas_call(main_kernel, out_shape=(jax.ShapeDtypeStruct((levels, colu...]
    while x217 -> x0, other arithmetic: 43.2 us -> none
    reduce_sum x30 -> x0, other arithmetic: 42.6 us -> none  [the longest x7 26.7 us: one_block(): jnp.sum(final_down, 0)]
    mul x8 -> x0, local copies, waits for them, and re-layouts: 37.7 us -> none  [the longest x7 37.5 us: column_physics(): quantity_bundle[2:, None] * expansion_modes[None] * slab_weight_per_area]
    add x21 -> x0, other arithmetic: 33.9 us -> none  [the longest x7 23.6 us: one_block(): transmit = extinct + reflect]
    mul x16 -> x1, other arithmetic: 24.3 us -> 0.76 us  [local(): 0.5 * rayleigh]
  transfers between devices with their start and end apart: 2 -> 1, of which waited for: 2 -> 1; matrix products, arithmetic and copies ran while one was open for 0% -> 3% of each run, Pallas kernels for 0% -> 0%
where the time goes in v1:
time: 95.2 us; the launch traced here: 94.8 us
  Pallas kernels  57.1 us (60%)
  blocking collectives  14.1 us (15%)
  starting transfers between devices  11.5 us (12%)
  waiting for transfers between devices  6.57 us (7%)
  local copies, waits for them, and re-layouts  3.9 us (4%)
  other arithmetic  0.98 us (1%)
    pallas_call x1, Pallas kernels, local(): pl.pallas_call(main_kernel, out_shape=(jax.ShapeDtypeStruct((levels, colu...  53.9 us
    all_to_all x1, blocking collectives, exchange(): lax.all_to_all(x.reshape(rows, 1, LANES), AXES, split_axis=0, concat_axis...  14.1 us
    all_to_all x1, starting transfers between devices, exchange(): lax.all_to_all(x.reshape(rows, 1, LANES), AXES, split_axis=0, concat_axis...  11.5 us
    all_to_all x1, waiting for transfers between devices, exchange(): lax.all_to_all(x.reshape(rows, 1, LANES), AXES, split_axis=0, concat_axis...  6.57 us
    unnamed x6, local copies, waits for them, and re-layouts  2.23 us
  transfers between devices with their start and end apart: 1, of which 1 were waited for; matrix products, arithmetic and copies ran while one was open for 3% of the time, Pallas kernels for 0%

profile of v1, /device:TPU:1, one launch (start us, length us, event | category | flops | bytes accessed | tf_op | source)
XLA Modules:
  0.0 94.8 jit_solution(12185035579472042871)
XLA Ops:
  0.6 1.4 %send.1 = f32[128,128]{1,0:T(8,128)} custom-call(f32[8,128]{1,0:T(8,128)} %bitcast.18, s32[8,128]{1,0:T(8,128)} %bitcast.19, f32[8,128]{1,0:T(8,128)} %bitcast.20), custom_call_target="tpu_custom_call" | custom-call | tf_op jit(solution)/shard_map/send/pallas_call | solution.py:298
  2.1 11.5 %all-to-all-start = ((f32[128,1,128]{2,1,0:T(1,128)}), f32[128,1,128]{2,1,0:T(1,128)S(1)}, u32[]{:S(2)}, u32[]{:S(2)}) async-start(f32[128,1,128]{2,1,0:T(1,128)} %bitcast.17), calls=%async_computation | async-start | bytes 131072 | tf_op jit(solution)/shard_map/all_to_all | solution.py:283
  13.6 0.8 broadcast_multiply_fusion
  14.4 0.8 concatenate.10
  15.2 0.1 fusion.1
  15.2 0.1 copy.22
  15.3 0.1 copy.23
  15.5 0.8 fusion.2
  16.3 0.1 broadcast_select_fusion
  16.4 0.1 pad_maximum_fusion.lhs_ref
  16.5 6.6 %all-to-all-done = f32[128,1,128]{2,1,0:T(1,128)S(1)} async-done(((f32[128,1,128]{2,1,0:T(1,128)}), f32[128,1,128]{2,1,0:T(1,128)S(1)}, u32[]{:S(2)}, u32[]{:S(2)}) %all-to-all-start) | async-done | bytes 65568 | tf_op jit(solution)/shard_map/all_to_all | solution.py:283
  23.1 0.0 copy-start
  23.1 1.3 %copy-done = f32[10,32,1024]{2,1,0:T(8,128)S(1)} copy-done((f32[10,32,1024]{2,1,0:T(8,128)S(1)}, f32[10,32,1024]{2,1,0:T(8,128)}, u32[]{:S(2)}) %copy-start) | copy-done | bytes 1310744
  24.4 0.0 copy-start.1
  24.4 0.7 copy-done.1
  25.1 53.9 %physics.1 = (f32[32,1024]{1,0:T(8,128)}, f32[128,128]{1,0:T(8,128)S(1)}) custom-call(s32[1]{0:T(128)} %bitcast.shift_ref, f32[10,32,1024]{2,1,0:T(8,128)S(1)} %copy-done, f32[128,128]{1,0:T(8,128)S(1)} %bitcast.13, s32[1,1024]{1,0:T(1,128)S(1)} %bitcast.15, bf16[112,80]{1,0:T(8,128)(2,1)S(1)} %pad_maximum_fusion.lhs_ref, ...), custom_call_target="tpu_custom_call" | custom-call | tf_op jit(solution)/shard_map/physics/pallas_call | solution.py:323
  79.0 14.1 %all_to_all.10 = f32[128,1,128]{2,1,0:T(1,128)} all-to-all(f32[128,1,128]{2,1,0:T(1,128)S(1)} %bitcast.14), channel_id=1, replica_groups=mesh['gx'=8,'gy'=16] {'gx','gy'}, dimensions={0} | all-to-all | bytes 131072 | tf_op jit(solution)/shard_map/all_to_all | solution.py:283
  93.1 1.7 %receive.1 = f32[3,1024]{1,0:T(4,128)} custom-call(f32[128,128]{1,0:T(8,128)} %bitcast.16), custom_call_target="tpu_custom_call" | custom-call | tf_op jit(solution)/shard_map/receive/pallas_call | solution.py:356
  (5 shorter events, 0.0 us)
Async XLA Ops:
  2.1 21.0 %all-to-all-start = ((f32[128,1,128]{2,1,0:T(1,128)}), f32[128,1,128]{2,1,0:T(1,128)S(1)}, u32[]{:S(2)}, u32[]{:S(2)}) async-start(f32[128,1,128]{2,1,0:T(1,128)} %bitcast.17), calls=%async_computation | async-start | bytes 131072 | tf_op jit(solution)/shard_map/all_to_all | solution.py:283
  23.1 1.3 %copy-start = (f32[10,32,1024]{2,1,0:T(8,128)S(1)}, f32[10,32,1024]{2,1,0:T(8,128)}, u32[]{:S(2)}) copy-start(f32[10,32,1024]{2,1,0:T(8,128)} %state_ref.1) | copy-start | bytes 3932164
  24.4 0.7 copy-start.1

commit v2 on v1

v2 whole, which is shorter than its diff:
```python
import jax
import jax.numpy as jnp
from jax import lax
from jax.experimental import pallas as pl
from jax.experimental.pallas import tpu as pltpu
from jax.sharding import PartitionSpec as P

AXES = ("gx", "gy")
F32 = jnp.float32
BF16 = jnp.bfloat16
LOG2E = 1.4426950408889634
DIFFUSIVITY = 1.66
HEAT_FACTOR = 8.0
LANES = 128
HALF = 64
UNROLL_DOWN = 8
UNROLL_RISE = 8
UNROLL_TAU = 8
CHUNK = 256


def split3(x):
    hi = x.astype(BF16)
    rest = x - hi.astype(F32)
    mid = rest.astype(BF16)
    low = (rest - mid.astype(F32)).astype(BF16)
    return hi, mid, low


def dot(a, b, dims=((1,), (0,))):
    return lax.dot_general(a, b, (dims, ((), ())), preferred_element_type=F32)


def iota(shape, dim):
    return lax.broadcasted_iota(jnp.int32, shape, dim)


def fetch(pairs, sems):
    copies = [pltpu.make_async_copy(a, b, sems.at[i]) for i, (a, b) in enumerate(pairs)]
    for c in copies:
        c.start()
    for c in copies:
        c.wait()


def send_kernel(cos_hbm, day_hbm, alb_hbm, out_ref, cos_ref, day_ref, alb_ref, sems):
    fetch(((cos_hbm, cos_ref), (day_hbm, day_ref), (alb_hbm, alb_ref)), sems)
    rows = cos_ref.shape[0]
    devices = out_ref.shape[0]
    group = devices // rows
    per = LANES // group
    keep = iota((devices, LANES), 1) // per == iota((devices, LANES), 0) % group
    cosine = jnp.where(day_ref[...] == 1, cos_ref[...], 0.0)

    def spread(x):
        x = jnp.broadcast_to(x[:, None, :], (rows, group, LANES)).reshape(devices, LANES)
        return jnp.where(keep, x, 0.0)

    out_ref[...] = spread(cosine) + pltpu.roll(spread(alb_ref[...]), per, 1)


def predictor_kernel(
    state_hbm,
    kdist_hbm,
    ray_hbm,
    solar_hbm,
    span_hbm,
    out_ref,
    lhs_ref,
    rayh_ref,
    sun_ref,
    owner_ref,
    slot_ref,
    state_ref,
    kdist_ref,
    ray_ref,
    solar_ref,
    span_ref,
    sems,
):
    pairs = (
        (kdist_hbm, kdist_ref),
        (ray_hbm, ray_ref),
        (solar_hbm, solar_ref),
        (span_hbm, span_ref),
        (state_hbm, state_ref),
    )
    fetch(pairs, sems)
    fields, levels, columns = state_ref.shape
    gases = fields - 2
    devices = owner_ref.shape[0]
    span = span_ref[...]
    hot = jnp.where(iota((devices, columns), 0) == span // columns, 1.0, 0.0)
    owner_ref[...] = hot.astype(BF16)
    slot_ref[...] = span % (columns // devices)

    def level(l, _):
        t = state_ref[0, pl.ds(l, 1), :] / 250.0
        m = state_ref[1, pl.ds(l, 1), :]
        q = jnp.concatenate([state_ref[2 + i, pl.ds(l, 1), :] for i in range(gases)], 0)
        modes = (None, t, t * t, 1.0 / t)
        v = [(q if b == 0 else q * modes[b]) * m for b in range(4)]
        at = pl.multiple_of(l * 4 * gases, 4 * gases)
        out_ref[pl.ds(at, 4 * gases), :] = jnp.concatenate(v, 0).astype(BF16)
        return 0

    lax.fori_loop(0, levels, level, 0, unroll=2)
    base = 4 * gases * levels
    for j, term in enumerate(split3(state_ref[1])):
        out_ref[pl.ds(base + j * levels, levels), :] = term

    npred, points = kdist_ref.shape
    rows = points // 2
    lane_low = iota((1, LANES), 1) < HALF
    source, target = iota((npred, npred), 0), iota((npred, npred), 1)
    move = jnp.where(source == target % gases * 4 + target // gases, 1.0, 0.0).astype(BF16)
    scale = -DIFFUSIVITY * LOG2E
    k1, k2, _ = split3(scale * dot(kdist_ref[...], move, ((0,), (0,))))

    def column(ref):
        return jnp.broadcast_to(ref[...], (LANES, points)).T

    ray = scale * column(ray_ref)
    r1, r2, r3 = (x.astype(F32)[:, :16] for x in split3(ray))
    place = iota((points, 16), 1)
    r = jnp.where(place == 2, r3, 0.0)
    r = jnp.where(jnp.logical_or(place == 1, place == 4), r2, r)
    r = jnp.where(jnp.logical_or(jnp.logical_or(place == 0, place == 3), place == 5), r1, r)
    terms = jnp.concatenate([k1.astype(F32), k2.astype(F32), r], 1)
    low, high = terms[:rows], terms[rows:]
    none = jnp.zeros_like(low)
    for k, pair in enumerate(((low, none), (high, none), (low, high))):
        lhs_ref[k] = jnp.concatenate(pair, 1).astype(BF16)

    for x, ref in ((0.5 * ray, rayh_ref), (column(solar_ref), sun_ref)):
        low, high = x[:rows], x[rows:]
        for k, y in enumerate((low, high, jnp.where(lane_low, low, high))):
            ref[2 * k] = y[: rows // 2]
            ref[2 * k + 1] = y[rows // 2 :]


def main_kernel(
    shift_ref,
    pred_ref,
    recv_ref,
    owner_ref,
    slot_ref,
    lhs_ref,
    rayh_ref,
    sun_ref,
    heat_ref,
    send_ref,
    extra_s,
    mass_s,
    pick_s,
    rhs_s,
    aux_s,
    tau0_s,
    tau1_s,
    trans_s,
    emit_s,
    back_s,
    net_s,
    sfc_s,
    out_s,
    fin_s,
):
    levels = heat_ref.shape[0]
    columns = pred_ref.shape[1]
    npred = pred_ref.shape[0] // levels - 3
    devices = recv_ref.shape[0]
    per = columns // devices
    part = rayh_ref.shape[1]
    base = npred * levels
    lane_low = iota((1, LANES), 1) < HALF
    half_rows = rhs_s.shape[2] // 2
    tau_s = (tau0_s, tau1_s)

    slot_hot = iota((per, columns), 0) == slot_ref[...]
    recv = pltpu.roll(recv_ref[...], shift_ref[0], 1).T[: 2 * per]
    sel = dot(jnp.concatenate(split3(recv), 0), owner_ref[...])
    sel = sel[: 2 * per] + sel[2 * per : 4 * per] + sel[4 * per :]
    cos_e = jnp.sum(jnp.where(slot_hot, sel[:per], 0.0), 0, keepdims=True)
    alb_e = jnp.sum(jnp.where(slot_hot, sel[per:], 0.0), 0, keepdims=True)
    extra = [x.astype(F32) for x in (*split3(cos_e), *split3(alb_e))]
    extra = jnp.concatenate(extra + [jnp.zeros((10, columns), F32)], 0)
    extra_s[...] = extra.astype(BF16)

    day = jnp.where(cos_e > 0.0, 1.0, 0.0)
    rows = columns // LANES
    day2 = jnp.concatenate([day[:, r * LANES : (r + 1) * LANES] for r in range(rows)], 0)
    upper = jnp.where(iota((LANES, LANES), 0) <= iota((LANES, LANES), 1), 1.0, 0.0)
    within = dot(day2.astype(BF16), upper.astype(BF16))
    place = []
    offset = jnp.zeros((1, 1), F32)
    for r in range(rows):
        place.append(within[r : r + 1] + offset)
        offset = offset + within[r : r + 1, LANES - 1 :]
    order = jnp.where(day > 0.0, jnp.concatenate(place, 1) - 1.0, -1.0).astype(jnp.int32)
    count = jnp.sum(day).astype(jnp.int32)
    chunks = (count + CHUNK - 1) // CHUNK
    units = (count + HALF - 1) // HALF

    def is_tail(unit):
        return jnp.logical_and(unit == units - 1, unit % 2 == 0)

    out_s[...] = jnp.zeros_like(out_s)
    fin_s[...] = jnp.zeros_like(fin_s)

    def gather(c, _):
        start = pl.multiple_of(c * CHUNK, CHUNK)
        hot = jnp.where(iota((CHUNK, columns), 0) + start == order, 1.0, 0.0).astype(BF16)
        pick_s[pl.ds(start, CHUNK), :] = hot
        out = dot(pred_ref[...], hot, ((1,), (1,)))
        more = dot(extra_s[...], hot, ((1,), (1,)))
        sub = iota((16, LANES), 0)
        for j in range(CHUNK // LANES):
            chunk = c * (CHUNK // LANES) + j
            piece = out[:, j * LANES : (j + 1) * LANES]
            ms = [piece[base + k * levels : base + (k + 1) * levels] for k in range(3)]
            for k in range(3):
                mass_s[k] = ms[k]
            ex = more[:8, j * LANES : (j + 1) * LANES]
            cosine = ex[0:1] + ex[1:2] + ex[2:3]
            albedo = ex[3:4] + ex[4:5] + ex[5:6]
            aux = jnp.concatenate(
                [ms[0] + ms[1] + ms[2], cosine, albedo, jnp.ones((6, LANES), F32)], 0
            )
            tail = is_tail(2 * chunk)
            aux_s[chunk] = jnp.where(
                jnp.logical_or(lane_low, jnp.logical_not(tail)), aux, pltpu.roll(aux, HALF, 1)
            )
            for l in range(levels):
                x = piece[l * npred : (l + 1) * npred].astype(BF16)
                rows = [mass_s[k, pl.ds(l, 1), :] for k in range(3)]
                y = jnp.where(sub < 3, rows[0], jnp.where(sub < 5, rows[1], rows[2]))
                y = jnp.where(sub < 6, y, 0.0).astype(BF16)
                at = pl.ds(l % 2 * LANES, LANES)
                rhs_s[chunk, l // 2, pl.ds(0, npred), at] = x
                rhs_s[chunk, l // 2, pl.ds(npred, npred), at] = x
                rhs_s[chunk, l // 2, pl.ds(2 * npred, 16), at] = y
                rhs_s[chunk, l // 2, pl.ds(half_rows, half_rows), at] = jnp.zeros(
                    (half_rows, LANES), BF16
                )

            @pl.when(tail)
            def _():
                def pair(l, _):
                    for j in range(2):
                        at = pl.ds(j * LANES, LANES)
                        x = rhs_s[chunk, l, pl.ds(0, half_rows), at].astype(F32)
                        low = jnp.where(lane_low, x, 0.0)
                        high = pltpu.roll(low, HALF, 1)
                        rhs_s[chunk, l, :, at] = jnp.concatenate([low, high], 0).astype(BF16)
                    return 0

                lax.fori_loop(0, levels // 2, pair, 0, unroll=2)

        return 0

    lax.fori_loop(0, chunks, gather, 0)

    def fold(x):
        return jnp.sum(x.reshape(x.shape[0] // 8, 8, LANES), 0)

    def where_is(unit):
        kind = jnp.where(is_tail(unit), 2, unit % 2)
        return unit // 2, kind

    def one(unit, slot):
        chunk, kind = where_is(unit)
        g = 2 * kind + slot
        now = tau_s[slot]
        cosine = aux_s[chunk, pl.ds(levels, 1), :]
        albedo = aux_s[chunk, pl.ds(levels + 1, 1), :]
        slope = 1.0 / (DIFFUSIVITY * cosine)

        if slot == 0:

            def optical(l, _):
                out = dot(lhs_ref[kind], rhs_s[chunk, l])
                for s in range(2):
                    for j in range(2):
                        tau_s[s][2 * l + j] = out[s * part : (s + 1) * part, j * LANES : (j + 1) * LANES]
                return 0

            lax.fori_loop(0, levels // 2, optical, 0, unroll=UNROLL_TAU)

            @pl.when(kind != 1)
            def _():
                net_s[...] = jnp.zeros_like(net_s)
                sfc_s[...] = jnp.zeros_like(sfc_s)

        def down(l, carry):
            back, emit, direct = carry
            net_s[l] += fold(direct + emit)
            tau = now[l]
            ext = jnp.exp2(tau)
            beam = jnp.exp2(tau * slope)
            half_w = rayh_ref[g] * aux_s[chunk, pl.ds(l, 1), :] * pl.reciprocal(tau)
            reflect = half_w * (1.0 - ext)
            transmit = ext + reflect
            lower = direct * beam
            source = half_w * (direct - lower)
            inv = pl.reciprocal(1.0 - reflect * back)
            trans = transmit * inv
            trans_s[l] = trans
            emit_s[l] = (source + reflect * emit) * inv
            back_s[l] = back
            new_back = reflect + (transmit * back) * trans
            new_emit = source + trans * (emit + back * source)
            return new_back, new_emit, lower

        zero = jnp.zeros((part, LANES), F32)
        back, emit, direct = lax.fori_loop(
            0, levels, down, (zero, zero, sun_ref[g] * cosine), unroll=UNROLL_DOWN
        )
        up = albedo * (emit + direct) * pl.reciprocal(1.0 - albedo * back)
        dif = emit + back * up
        sfc_s[0] += fold(direct)
        sfc_s[1] += fold(dif)
        net_s[levels] += fold(direct + dif - up)

        def rise(j, up):
            l = levels - 1 - j
            up = trans_s[l] * up + emit_s[l]
            net_s[l] -= fold(up - back_s[l] * up)
            return up

        up = lax.fori_loop(0, levels, rise, up, unroll=UNROLL_RISE)
        sfc_s[2] += fold(up)

        if slot == 0:
            return

        @pl.when(kind != 0)
        def _():
            net = jnp.sum(net_s[...], 1)
            heat = HEAT_FACTOR * (net[:levels] - net[1:])
            out = jnp.concatenate([heat, jnp.sum(sfc_s[...], 1), jnp.zeros((5, LANES), F32)], 0)
            out = jnp.where(kind == 2, out + pltpu.roll(out, HALF, 1), out)
            mass = aux_s[chunk, pl.ds(0, levels), :]
            out = out / jnp.concatenate([mass, jnp.ones((8, LANES), F32)], 0)
            out_s[chunk] = jnp.where(iota((1, LANES), 1) + chunk * LANES < count, out, 0.0)

    def both(unit, _):
        one(unit, 0)
        one(unit, 1)
        return 0

    lax.fori_loop(0, units, both, 0)

    def spread(c, _):
        two = jnp.concatenate([out_s[(CHUNK // LANES) * c + j] for j in range(CHUNK // LANES)], 1)
        rows = two.shape[0]
        back = dot(
            jnp.concatenate([x.astype(F32) for x in split3(two)], 0).astype(BF16),
            pick_s[pl.ds(pl.multiple_of(c * CHUNK, CHUNK), CHUNK), :],
        )
        fin_s[...] += back[:rows] + back[rows : 2 * rows] + back[2 * rows :]
        return 0

    lax.fori_loop(0, chunks, spread, 0)

    heat_ref[...] = fin_s[pl.ds(0, levels), :]
    sfc = fin_s[pl.ds(levels, 8), :]
    vals = jnp.concatenate([jnp.where(slot_hot, sfc[q : q + 1], 0.0) for q in range(3)], 0)
    hot = owner_ref[...]
    send = sum(dot(hot, x, ((1,), (1,))) for x in split3(vals))
    send_ref[...] = jnp.concatenate([send, jnp.zeros((devices, LANES - 3 * per), F32)], 1)


def recv_kernel(recv_ref, out_ref):
    devices = recv_ref.shape[0]
    width = out_ref.shape[1]
    per = width // devices
    group = LANES // per
    lane = iota((LANES, 3 * LANES), 1)
    hot = jnp.where(iota((LANES, 3 * LANES), 0) == lane // LANES * per + lane % per, 1.0, 0.0)
    hot = hot.astype(BF16)
    x = sum(dot(term, hot) for term in split3(recv_ref[...]))
    shape = (devices, 3 * LANES)
    x = jnp.where(iota(shape, 1) % LANES // per == iota(shape, 0) % group, x, 0.0)
    x = jnp.sum(x.reshape(devices // group, group, 3 * LANES), 1)
    for q in range(3):
        for r in range(devices // group):
            out_ref[q : q + 1, r * LANES : (r + 1) * LANES] = x[
                r : r + 1, q * LANES : (q + 1) * LANES
            ]


def exchange(x):
    rows = x.shape[0]
    y = lax.all_to_all(
        x.reshape(rows, 1, LANES), AXES, split_axis=0, concat_axis=0, tiled=True
    )
    return y.reshape(rows, LANES)


def in_hbm(x):
    return pltpu.with_memory_space_constraint(x, pltpu.HBM)


def local(state, kdist, rayleigh, solar, span_map, cos_zenith, day_flag, albedo):
    fields, levels, columns = state.shape
    devices = lax.axis_size(AXES)
    per = columns // devices
    group = LANES // per
    rows = columns // LANES
    npred = kdist.shape[1]
    grows = kdist.shape[0] // 2

    hbm = pl.BlockSpec(memory_space=pltpu.HBM)
    sent = pl.pallas_call(
        send_kernel,
        out_shape=jax.ShapeDtypeStruct((devices, LANES), F32),
        in_specs=[hbm] * 3,
        scratch_shapes=[
            pltpu.VMEM((rows, LANES), F32),
            pltpu.VMEM((rows, LANES), jnp.int32),
            pltpu.VMEM((rows, LANES), F32),
            pltpu.SemaphoreType.DMA((3,)),
        ],
        compiler_params=pltpu.CompilerParams(vmem_limit_bytes=4 << 20),
        name="send",
    )(
        in_hbm(cos_zenith.reshape(rows, LANES)),
        in_hbm(day_flag.reshape(rows, LANES)),
        in_hbm(albedo.reshape(rows, LANES)),
    )
    recv = exchange(sent)
    points = 2 * grows
    preds, lhs, rayh, sun, owner, slot = pl.pallas_call(
        predictor_kernel,
        out_shape=(
            jax.ShapeDtypeStruct(((npred + 3) * levels, columns), BF16),
            jax.ShapeDtypeStruct((3, grows, 4 * npred + 32), BF16),
            jax.ShapeDtypeStruct((6, grows // 2, LANES), F32),
            jax.ShapeDtypeStruct((6, grows // 2, LANES), F32),
            jax.ShapeDtypeStruct((devices, columns), BF16),
            jax.ShapeDtypeStruct((1, columns), jnp.int32),
        ),
        in_specs=[hbm] * 5,
        scratch_shapes=[
            pltpu.VMEM((fields, levels, columns), F32),
            pltpu.VMEM((npred, points), BF16),
            pltpu.VMEM((1, points), F32),
            pltpu.VMEM((1, points), F32),
            pltpu.VMEM((1, columns), jnp.int32),
            pltpu.SemaphoreType.DMA((5,)),
        ],
        compiler_params=pltpu.CompilerParams(vmem_limit_bytes=12 << 20),
        name="predictors",
    )(
        in_hbm(state),
        in_hbm(kdist.T),
        in_hbm(rayleigh.reshape(1, -1)),
        in_hbm(solar.reshape(1, -1)),
        in_hbm(span_map.reshape(1, columns)),
    )
    shift = (LANES - lax.axis_index(AXES) % group * per) % LANES
    chunks = columns // LANES
    g_array = pltpu.VMEM((levels, grows // 2, LANES), F32)
    vmem = pl.BlockSpec(memory_space=pltpu.VMEM)
    heating, back = pl.pallas_call(
        main_kernel,
        out_shape=(
            jax.ShapeDtypeStruct((levels, columns), F32),
            jax.ShapeDtypeStruct((devices, LANES), F32),
        ),
        in_specs=[pl.BlockSpec(memory_space=pltpu.SMEM)] + [vmem] * 7,
        out_specs=(vmem, vmem),
        scratch_shapes=[
            pltpu.VMEM((16, columns), BF16),
            pltpu.VMEM((3, levels, LANES), F32),
            pltpu.VMEM((columns, columns), BF16),
            pltpu.VMEM((chunks, levels // 2, lhs.shape[2], 2 * LANES), BF16),
            pltpu.VMEM((chunks, levels + 8, LANES), F32),
            g_array,
            g_array,
            g_array,
            g_array,
            g_array,
            pltpu.VMEM((levels + 1, 8, LANES), F32),
            pltpu.VMEM((3, 8, LANES), F32),
            pltpu.VMEM((chunks, levels + 8, LANES), F32),
            pltpu.VMEM((levels + 8, columns), F32),
        ],
        compiler_params=pltpu.CompilerParams(vmem_limit_bytes=26 << 20),
        name="physics",
    )(
        shift.reshape(1).astype(jnp.int32),
        preds,
        recv,
        owner,
        slot,
        lhs,
        rayh,
        sun,
    )
    surface = pl.pallas_call(
        recv_kernel,
        out_shape=jax.ShapeDtypeStruct((3, columns), F32),
        compiler_params=pltpu.CompilerParams(vmem_limit_bytes=4 << 20),
        name="receive",
    )(exchange(back))
    return heating, surface


def solution(mesh):
    cols = P(AXES)
    in_specs = (P(None, None, AXES), P(), P(), P(), cols, cols, cols, cols)
    out_specs = (P(None, AXES), P(None, AXES))
    return jax.shard_map(
        local, mesh=mesh, in_specs=in_specs, out_specs=out_specs, check_vma=False
    )
```

time: 95.2 us -> 70.7 us (0.74)
  Pallas kernels: 57.1 us -> 38.3 us
  local copies, waits for them, and re-layouts: 3.9 us -> 0 us
  other arithmetic: 0.98 us -> 0 us
    pallas_call x1, Pallas kernels: 53.9 us -> 32.8 us  [local(): pl.pallas_call(main_kernel, out_shape=(jax.ShapeDtypeStruct((levels, colu...]
    pallas_call x0 -> x1, Pallas kernels: none -> 3.19 us  [local(): pl.pallas_call(predictor_kernel, out_shape=(jax.ShapeDtypeStruct(((npred...]
    unnamed x6 -> x0, local copies, waits for them, and re-layouts: 2.23 us -> none
  transfers between devices with their start and end apart: 1 -> 1, of which waited for: 1 -> 1; matrix products, arithmetic and copies ran while one was open for 3% -> 0% of each run, Pallas kernels for 0% -> 5%
where the time goes in v2:
time: 70.7 us
  Pallas kernels  38.3 us (54%)
  blocking collectives  13.9 us (20%)
  starting transfers between devices  11.5 us (16%)
  waiting for transfers between devices  6.3 us (9%)
    pallas_call x1, Pallas kernels, local(): pl.pallas_call(main_kernel, out_shape=(jax.ShapeDtypeStruct((levels, colu...  32.8 us
    all_to_all x1, blocking collectives, exchange(): lax.all_to_all(x.reshape(rows, 1, LANES), AXES, split_axis=0, concat_axis...  13.9 us
    all_to_all x1, starting transfers between devices, exchange(): lax.all_to_all(x.reshape(rows, 1, LANES), AXES, split_axis=0, concat_axis...  11.5 us
    all_to_all x1, waiting for transfers between devices, exchange(): lax.all_to_all(x.reshape(rows, 1, LANES), AXES, split_axis=0, concat_axis...  6.3 us
    pallas_call x1, Pallas kernels, local(): pl.pallas_call(predictor_kernel, out_shape=(jax.ShapeDtypeStruct(((npred...  3.19 us
    pallas_call x1, Pallas kernels, local(): pl.pallas_call(send_kernel, out_shape=jax.ShapeDtypeStruct((devices, LANE...  1.47 us
  transfers between devices with their start and end apart: 1, of which 1 were waited for; matrix products, arithmetic and copies ran while one was open for 0% of the time, Pallas kernels for 5%

profile of v2, /device:TPU:1, one launch (start us, length us, event | category | flops | bytes accessed | tf_op | source)
XLA Modules:
  0.0 70.7 jit_solution(7811995883312685089)
XLA Ops:
  0.6 1.5 %send.1 = f32[128,128]{1,0:T(8,128)} custom-call(f32[8,128]{1,0:T(8,128)} %bitcast.21, s32[8,128]{1,0:T(8,128)} %bitcast.22, f32[8,128]{1,0:T(8,128)} %bitcast.23), custom_call_target="tpu_custom_call" | custom-call | tf_op jit(solution)/shard_map/send/pallas_call | solution.py:414
  2.1 11.5 %all-to-all-start = ((f32[128,1,128]{2,1,0:T(1,128)}), f32[128,1,128]{2,1,0:T(1,128)S(1)}, u32[]{:S(2)}, u32[]{:S(2)}) async-start(f32[128,1,128]{2,1,0:T(1,128)} %bitcast.9), calls=%async_computation | async-start | bytes 131072 | tf_op jit(solution)/shard_map/all_to_all | solution.py:394
  13.6 3.2 %predictors.1 = (bf16[1120,1024]{1,0:T(8,128)(2,1)S(1)}, bf16[3,112,160]{2,1,0:T(8,128)(2,1)S(1)}, f32[6,56,128]{2,1,0:T(8,128)S(1)}, f32[6,56,128]{2,1,0:T(8,12...) custom-call(f32[10,32,1024]{2,1,0:T(8,128)} %state_hbm.1, bf16[32,224]{1,0:T(8,128)(2,1)} %bitcast.19, ...), custom_call_target="tpu_custom_call" | custom-call | tf_op jit(solution)/shard_map/predictors/pallas_call | solution.py:433
  16.8 6.3 %all-to-all-done = f32[128,1,128]{2,1,0:T(1,128)S(1)} async-done(((f32[128,1,128]{2,1,0:T(1,128)}), f32[128,1,128]{2,1,0:T(1,128)S(1)}, u32[]{:S(2)}, u32[]{:S(2)}) %all-to-all-start) | async-done | bytes 65568 | tf_op jit(solution)/shard_map/all_to_all | solution.py:394
  23.1 32.8 %physics.1 = (f32[32,1024]{1,0:T(8,128)}, f32[128,128]{1,0:T(8,128)S(1)}) custom-call(s32[1]{0:T(128)} %bitcast.shift_ref, bf16[1120,1024]{1,0:T(8,128)(2,1)S(1)} %get-tuple-element.10.pred_ref, f32[128,128]{1,0:T(8,128)S(1)} %bitcast.17, bf16[128,1024]{1,0:T(8,128)(2,1)S(1)} %get-tuple-element.11.owner_ref, s32[1,1024]{1,0:T(1,128)S(1)} %get-tuple-element.12.slot_ref, ...), custom_call_target="tpu_custom_call" | custom-call | tf_op jit(solution)/shard_map/physics/pallas_call | solution.py:465
  55.9 13.9 %all_to_all.10 = f32[128,1,128]{2,1,0:T(1,128)S(1)} all-to-all(f32[128,1,128]{2,1,0:T(1,128)S(1)} %bitcast.18), channel_id=1, replica_groups=mesh['gx'=8,'gy'=16] {'gx','gy'}, dimensions={0} | all-to-all | bytes 131072 | tf_op jit(solution)/shard_map/all_to_all | solution.py:394
  69.8 0.9 %receive.1 = f32[3,1024]{1,0:T(4,128)} custom-call(f32[128,128]{1,0:T(8,128)S(1)} %bitcast.16), custom_call_target="tpu_custom_call" | custom-call | tf_op jit(solution)/shard_map/receive/pallas_call | solution.py:501
Async XLA Ops:
  2.1 21.0 %all-to-all-start = ((f32[128,1,128]{2,1,0:T(1,128)}), f32[128,1,128]{2,1,0:T(1,128)S(1)}, u32[]{:S(2)}, u32[]{:S(2)}) async-start(f32[128,1,128]{2,1,0:T(1,128)} %bitcast.9), calls=%async_computation | async-start | bytes 131072 | tf_op jit(solution)/shard_map/all_to_all | solution.py:394

commit v3 on v2

--- a/solution.py
+++ b/solution.py
@@ -13,8 +13,8 @@
 HEAT_FACTOR = 8.0
 LANES = 128
 HALF = 64
-UNROLL_DOWN = 8
-UNROLL_RISE = 8
+UNROLL_DOWN = 16
+UNROLL_RISE = 32
 UNROLL_TAU = 8
 CHUNK = 256
 
@@ -67,6 +67,7 @@
     span_hbm,
     out_ref,
     lhs_ref,
+    tail_ref,
     rayh_ref,
     sun_ref,
     owner_ref,
@@ -128,9 +129,8 @@
     r = jnp.where(jnp.logical_or(jnp.logical_or(place == 0, place == 3), place == 5), r1, r)
     terms = jnp.concatenate([k1.astype(F32), k2.astype(F32), r], 1)
     low, high = terms[:rows], terms[rows:]
-    none = jnp.zeros_like(low)
-    for k, pair in enumerate(((low, none), (high, none), (low, high))):
-        lhs_ref[k] = jnp.concatenate(pair, 1).astype(BF16)
+    lhs_ref[...] = terms.astype(BF16)
+    tail_ref[...] = jnp.concatenate([low, high], 1).astype(BF16)
 
     for x, ref in ((0.5 * ray, rayh_ref), (column(solar_ref), sun_ref)):
         low, high = x[:rows], x[rows:]
@@ -146,17 +146,19 @@
     owner_ref,
     slot_ref,
     lhs_ref,
+    tail_ref,
     rayh_ref,
     sun_ref,
     heat_ref,
     send_ref,
     extra_s,
+    picked_s,
     mass_s,
     pick_s,
     rhs_s,
     aux_s,
-    tau0_s,
-    tau1_s,
+    tau_s,
+    half_s,
     trans_s,
     emit_s,
     back_s,
@@ -174,7 +176,6 @@
     base = npred * levels
     lane_low = iota((1, LANES), 1) < HALF
     half_rows = rhs_s.shape[2] // 2
-    tau_s = (tau0_s, tau1_s)
 
     slot_hot = iota((per, columns), 0) == slot_ref[...]
     recv = pltpu.roll(recv_ref[...], shift_ref[0], 1).T[: 2 * per]
@@ -198,6 +199,9 @@
         offset = offset + within[r : r + 1, LANES - 1 :]
     order = jnp.where(day > 0.0, jnp.concatenate(place, 1) - 1.0, -1.0).astype(jnp.int32)
     count = jnp.sum(day).astype(jnp.int32)
+    before = [jnp.int32(0)]
+    for k in range(columns // CHUNK):
+        before.append(before[-1] + jnp.sum(day[:, k * CHUNK : (k + 1) * CHUNK]).astype(jnp.int32))
     chunks = (count + CHUNK - 1) // CHUNK
     units = (count + HALF - 1) // HALF
 
@@ -211,16 +215,30 @@
         start = pl.multiple_of(c * CHUNK, CHUNK)
         hot = jnp.where(iota((CHUNK, columns), 0) + start == order, 1.0, 0.0).astype(BF16)
         pick_s[pl.ds(start, CHUNK), :] = hot
-        out = dot(pred_ref[...], hot, ((1,), (1,)))
-        more = dot(extra_s[...], hot, ((1,), (1,)))
+        for k in range(columns // CHUNK):
+            at = slice(k * CHUNK, (k + 1) * CHUNK)
+
+            def part_of():
+                rows = jnp.concatenate([pred_ref[:, at], extra_s[:, at]], 0)
+                return dot(rows, pick_s[pl.ds(start, CHUNK), at], ((1,), (1,)))
+
+            @pl.when(jnp.logical_and(before[k] <= start, before[k + 1] > start))
+            def _():
+                picked_s[...] = part_of()
+
+            @pl.when(jnp.logical_and(before[k] > start, before[k] < start + CHUNK))
+            def _():
+                picked_s[...] += part_of()
+
         sub = iota((16, LANES), 0)
         for j in range(CHUNK // LANES):
             chunk = c * (CHUNK // LANES) + j
-            piece = out[:, j * LANES : (j + 1) * LANES]
-            ms = [piece[base + k * levels : base + (k + 1) * levels] for k in range(3)]
+            lanes = slice(j * LANES, (j + 1) * LANES)
+            piece = picked_s.at[:, lanes]
+            ms = [piece[base + k * levels : base + (k + 1) * levels, :] for k in range(3)]
             for k in range(3):
                 mass_s[k] = ms[k]
-            ex = more[:8, j * LANES : (j + 1) * LANES]
+            ex = piece[base + 3 * levels : base + 3 * levels + 8, :]
             cosine = ex[0:1] + ex[1:2] + ex[2:3]
             albedo = ex[3:4] + ex[4:5] + ex[5:6]
             aux = jnp.concatenate(
@@ -231,7 +249,7 @@
                 jnp.logical_or(lane_low, jnp.logical_not(tail)), aux, pltpu.roll(aux, HALF, 1)
             )
             for l in range(levels):
-                x = piece[l * npred : (l + 1) * npred].astype(BF16)
+                x = piece[l * npred : (l + 1) * npred, :].astype(BF16)
                 rows = [mass_s[k, pl.ds(l, 1), :] for k in range(3)]
                 y = jnp.where(sub < 3, rows[0], jnp.where(sub < 5, rows[1], rows[2]))
                 y = jnp.where(sub < 6, y, 0.0).astype(BF16)
@@ -239,19 +257,16 @@
                 rhs_s[chunk, l // 2, pl.ds(0, npred), at] = x
                 rhs_s[chunk, l // 2, pl.ds(npred, npred), at] = x
                 rhs_s[chunk, l // 2, pl.ds(2 * npred, 16), at] = y
-                rhs_s[chunk, l // 2, pl.ds(half_rows, half_rows), at] = jnp.zeros(
-                    (half_rows, LANES), BF16
-                )
 
             @pl.when(tail)
             def _():
                 def pair(l, _):
                     for j in range(2):
                         at = pl.ds(j * LANES, LANES)
-                        x = rhs_s[chunk, l, pl.ds(0, half_rows), at].astype(F32)
-                        low = jnp.where(lane_low, x, 0.0)
-                        high = pltpu.roll(low, HALF, 1)
-                        rhs_s[chunk, l, :, at] = jnp.concatenate([low, high], 0).astype(BF16)
+                        x = rhs_s[chunk, l, pl.ds(npred, npred + 16), at].astype(F32)
+                        x = pltpu.roll(x, HALF, 1).astype(BF16)
+                        rhs_s[chunk, l, pl.ds(half_rows, npred), at] = x[:npred]
+                        rhs_s[chunk, l, pl.ds(half_rows + npred, npred + 16), at] = x
                     return 0
 
                 lax.fori_loop(0, levels // 2, pair, 0, unroll=2)
@@ -270,21 +285,36 @@
     def one(unit, slot):
         chunk, kind = where_is(unit)
         g = 2 * kind + slot
-        now = tau_s[slot]
+        now = tau_s.at[2 * (kind % 2) + slot]
+        half = half_s.at[2 * (kind % 2) + slot]
         cosine = aux_s[chunk, pl.ds(levels, 1), :]
         albedo = aux_s[chunk, pl.ds(levels + 1, 1), :]
         slope = 1.0 / (DIFFUSIVITY * cosine)
 
         if slot == 0:
 
-            def optical(l, _):
-                out = dot(lhs_ref[kind], rhs_s[chunk, l])
-                for s in range(2):
-                    for j in range(2):
-                        tau_s[s][2 * l + j] = out[s * part : (s + 1) * part, j * LANES : (j + 1) * LANES]
+            def keep(l, out, first):
+                for j in range(2):
+                    mass = aux_s[chunk, pl.ds(2 * l + j, 1), :]
+                    for s in range(out.shape[0] // part):
+                        y = out[s * part : (s + 1) * part, j * LANES : (j + 1) * LANES]
+                        tau_s[s, 2 * l + j] = y
+                        half_s[s, 2 * l + j] = rayh_ref[first + s] * mass * pl.reciprocal(y)
                 return 0
 
-            lax.fori_loop(0, levels // 2, optical, 0, unroll=UNROLL_TAU)
+            @pl.when(kind == 0)
+            def _():
+                def pair(l, _):
+                    return keep(l, dot(lhs_ref[...], rhs_s[chunk, l, :half_rows]), 0)
+
+                lax.fori_loop(0, levels // 2, pair, 0, unroll=UNROLL_TAU)
+
+            @pl.when(kind == 2)
+            def _():
+                def pair(l, _):
+                    return keep(l, dot(tail_ref[...], rhs_s[chunk, l]), 4)
+
+                lax.fori_loop(0, levels // 2, pair, 0, unroll=UNROLL_TAU)
 
             @pl.when(kind != 1)
             def _():
@@ -297,7 +327,7 @@
             tau = now[l]
             ext = jnp.exp2(tau)
             beam = jnp.exp2(tau * slope)
-            half_w = rayh_ref[g] * aux_s[chunk, pl.ds(l, 1), :] * pl.reciprocal(tau)
+            half_w = half[l]
             reflect = half_w * (1.0 - ext)
             transmit = ext + reflect
             lower = direct * beam
@@ -430,11 +460,12 @@
     )
     recv = exchange(sent)
     points = 2 * grows
-    preds, lhs, rayh, sun, owner, slot = pl.pallas_call(
+    preds, lhs, tail, rayh, sun, owner, slot = pl.pallas_call(
         predictor_kernel,
         out_shape=(
             jax.ShapeDtypeStruct(((npred + 3) * levels, columns), BF16),
-            jax.ShapeDtypeStruct((3, grows, 4 * npred + 32), BF16),
+            jax.ShapeDtypeStruct((points, 2 * npred + 16), BF16),
+            jax.ShapeDtypeStruct((grows, 4 * npred + 32), BF16),
             jax.ShapeDtypeStruct((6, grows // 2, LANES), F32),
             jax.ShapeDtypeStruct((6, grows // 2, LANES), F32),
             jax.ShapeDtypeStruct((devices, columns), BF16),
@@ -468,16 +499,17 @@
             jax.ShapeDtypeStruct((levels, columns), F32),
             jax.ShapeDtypeStruct((devices, LANES), F32),
         ),
-        in_specs=[pl.BlockSpec(memory_space=pltpu.SMEM)] + [vmem] * 7,
+        in_specs=[pl.BlockSpec(memory_space=pltpu.SMEM)] + [vmem] * 8,
         out_specs=(vmem, vmem),
         scratch_shapes=[
             pltpu.VMEM((16, columns), BF16),
+            pltpu.VMEM(((npred + 3) * levels + 16, CHUNK), F32),
             pltpu.VMEM((3, levels, LANES), F32),
             pltpu.VMEM((columns, columns), BF16),
-            pltpu.VMEM((chunks, levels // 2, lhs.shape[2], 2 * LANES), BF16),
+            pltpu.VMEM((chunks, levels // 2, tail.shape[1], 2 * LANES), BF16),
             pltpu.VMEM((chunks, levels + 8, LANES), F32),
-            g_array,
-            g_array,
+            pltpu.VMEM((4, levels, grows // 2, LANES), F32),
+            pltpu.VMEM((4, levels, grows // 2, LANES), F32),
             g_array,
             g_array,
             g_array,
@@ -486,7 +518,7 @@
             pltpu.VMEM((chunks, levels + 8, LANES), F32),
             pltpu.VMEM((levels + 8, columns), F32),
         ],
-        compiler_params=pltpu.CompilerParams(vmem_limit_bytes=26 << 20),
+        compiler_params=pltpu.CompilerParams(vmem_limit_bytes=34 << 20),
         name="physics",
     )(
         shift.reshape(1).astype(jnp.int32),
@@ -495,6 +527,7 @@
         owner,
         slot,
         lhs,
+        tail,
         rayh,
         sun,
     )

time: 70.7 us -> 65.6 us (0.928)
  Pallas kernels: 38.3 us -> 33.1 us
    pallas_call x1, Pallas kernels: 32.8 us -> 27.6 us  [local(): pl.pallas_call(main_kernel, out_shape=(jax.ShapeDtypeStruct((levels, colu...]
where the time goes in v3:
time: 65.6 us; the launch traced here: 65 us
  Pallas kernels  33.1 us (50%)
  blocking collectives  13.4 us (20%)
  starting transfers between devices  11.5 us (18%)
  waiting for transfers between devices  6.31 us (10%)
  between operations  0.69 us (1%)
    pallas_call x1, Pallas kernels, local(): pl.pallas_call(main_kernel, out_shape=(jax.ShapeDtypeStruct((levels, colu...  27.6 us
    all_to_all x1, blocking collectives, exchange(): lax.all_to_all(x.reshape(rows, 1, LANES), AXES, split_axis=0, concat_axis...  13.4 us
    all_to_all x1, starting transfers between devices, exchange(): lax.all_to_all(x.reshape(rows, 1, LANES), AXES, split_axis=0, concat_axis...  11.5 us
    all_to_all x1, waiting for transfers between devices, exchange(): lax.all_to_all(x.reshape(rows, 1, LANES), AXES, split_axis=0, concat_axis...  6.31 us
    pallas_call x1, Pallas kernels, local(): pl.pallas_call(predictor_kernel, out_shape=(jax.ShapeDtypeStruct(((npred...  3.18 us
    pallas_call x1, Pallas kernels, local(): pl.pallas_call(send_kernel, out_shape=jax.ShapeDtypeStruct((devices, LANE...  1.47 us
  transfers between devices with their start and end apart: 1, of which 1 were waited for; matrix products, arithmetic and copies ran while one was open for 0% of the time, Pallas kernels for 5%

profile of v3, /device:TPU:1, one launch (start us, length us, event | category | flops | bytes accessed | tf_op | source)
XLA Modules:
  0.0 65.0 jit_solution(8486019722295100090)
XLA Ops:
  0.6 1.5 %send.1 = f32[128,128]{1,0:T(8,128)} custom-call(f32[8,128]{1,0:T(8,128)} %bitcast.21, s32[8,128]{1,0:T(8,128)} %bitcast.22, f32[8,128]{1,0:T(8,128)} %bitcast.23), custom_call_target="tpu_custom_call" | custom-call | tf_op jit(solution)/shard_map/send/pallas_call | solution.py:444
  2.1 11.5 %all-to-all-start = ((f32[128,1,128]{2,1,0:T(1,128)}), f32[128,1,128]{2,1,0:T(1,128)S(1)}, u32[]{:S(2)}, u32[]{:S(2)}) async-start(f32[128,1,128]{2,1,0:T(1,128)} %bitcast.9), calls=%async_computation | async-start | bytes 131072 | tf_op jit(solution)/shard_map/all_to_all | solution.py:424
  13.6 3.2 %predictors.1 = (bf16[1120,1024]{1,0:T(8,128)(2,1)S(1)}, bf16[224,80]{1,0:T(8,128)(2,1)S(1)}, bf16[112,160]{1,0:T(8,128)(2,1)S(1)}, f32[6,56,128]{2,1,0:T(8,128)...) custom-call(f32[10,32,1024]{2,1,0:T(8,128)} %state_hbm.1, ...), custom_call_target="tpu_custom_call" | custom-call | tf_op jit(solution)/shard_map/predictors/pallas_call | solution.py:463
  16.8 6.3 %all-to-all-done = f32[128,1,128]{2,1,0:T(1,128)S(1)} async-done(((f32[128,1,128]{2,1,0:T(1,128)}), f32[128,1,128]{2,1,0:T(1,128)S(1)}, u32[]{:S(2)}, u32[]{:S(2)}) %all-to-all-start) | async-done | bytes 65568 | tf_op jit(solution)/shard_map/all_to_all | solution.py:424
  23.1 27.6 %physics.1 = (f32[32,1024]{1,0:T(8,128)}, f32[128,128]{1,0:T(8,128)S(1)}) custom-call(s32[1]{0:T(128)} %bitcast.shift_ref, bf16[1120,1024]{1,0:T(8,128)(2,1)S(1)} %get-tuple-element.11.pred_ref, f32[128,128]{1,0:T(8,128)S(1)} %bitcast.16, bf16[128,1024]{1,0:T(8,128)(2,1)S(1)} %get-tuple-element.12.owner_ref, s32[1,1024]{1,0:T(1,128)S(1)} %get-tuple-element.13.slot_ref, ...), custom_call_target="tpu_custom_call" | custom-call | tf_op jit(solution)/shard_map/physics/pallas_call | solution.py:496
  50.8 13.4 %all_to_all.10 = f32[128,1,128]{2,1,0:T(1,128)S(1)} all-to-all(f32[128,1,128]{2,1,0:T(1,128)S(1)} %bitcast.18), channel_id=1, replica_groups=mesh['gx'=8,'gy'=16] {'gx','gy'}, dimensions={0} | all-to-all | bytes 131072 | tf_op jit(solution)/shard_map/all_to_all | solution.py:424
  64.2 0.9 %receive.1 = f32[3,1024]{1,0:T(4,128)} custom-call(f32[128,128]{1,0:T(8,128)S(1)} %bitcast.17), custom_call_target="tpu_custom_call" | custom-call | tf_op jit(solution)/shard_map/receive/pallas_call | solution.py:534
Async XLA Ops:
  2.1 21.0 %all-to-all-start = ((f32[128,1,128]{2,1,0:T(1,128)}), f32[128,1,128]{2,1,0:T(1,128)S(1)}, u32[]{:S(2)}, u32[]{:S(2)}) async-start(f32[128,1,128]{2,1,0:T(1,128)} %bitcast.9), calls=%async_computation | async-start | bytes 131072 | tf_op jit(solution)/shard_map/all_to_all | solution.py:424

commit v4 on v3

--- a/solution.py
+++ b/solution.py
@@ -13,9 +13,9 @@
 HEAT_FACTOR = 8.0
 LANES = 128
 HALF = 64
-UNROLL_DOWN = 16
+UNROLL_DOWN = 32
 UNROLL_RISE = 32
-UNROLL_TAU = 8
+UNROLL_TAU = 16
 CHUNK = 256
 
 
@@ -396,7 +396,9 @@
     sfc = fin_s[pl.ds(levels, 8), :]
     vals = jnp.concatenate([jnp.where(slot_hot, sfc[q : q + 1], 0.0) for q in range(3)], 0)
     hot = owner_ref[...]
-    send = sum(dot(hot, x, ((1,), (1,))) for x in split3(vals))
+    terms = jnp.concatenate([x.astype(F32) for x in split3(vals)], 0).astype(BF16)
+    send = dot(hot, terms, ((1,), (1,)))
+    send = sum(send[:, j * 3 * per : (j + 1) * 3 * per] for j in range(3))
     send_ref[...] = jnp.concatenate([send, jnp.zeros((devices, LANES - 3 * per), F32)], 1)
 
 

time: 65.6 us -> 63.9 us (0.974)
  Pallas kernels: 33.1 us -> 31.5 us
    pallas_call x1, Pallas kernels: 27.6 us -> 26 us  [local(): pl.pallas_call(main_kernel, out_shape=(jax.ShapeDtypeStruct((levels, colu...]
where the time goes in v4:
time: 63.9 us; the launch traced here: 63.8 us
  Pallas kernels  31.5 us (49%)
  blocking collectives  13.9 us (22%)
  starting transfers between devices  11.5 us (18%)
  waiting for transfers between devices  6.31 us (10%)
  between operations  0.69 us (1%)
    pallas_call x1, Pallas kernels, local(): pl.pallas_call(main_kernel, out_shape=(jax.ShapeDtypeStruct((levels, colu...  26 us
    all_to_all x1, blocking collectives, exchange(): lax.all_to_all(x.reshape(rows, 1, LANES), AXES, split_axis=0, concat_axis...  13.9 us
    all_to_all x1, starting transfers between devices, exchange(): lax.all_to_all(x.reshape(rows, 1, LANES), AXES, split_axis=0, concat_axis...  11.5 us
    all_to_all x1, waiting for transfers between devices, exchange(): lax.all_to_all(x.reshape(rows, 1, LANES), AXES, split_axis=0, concat_axis...  6.31 us
    pallas_call x1, Pallas kernels, local(): pl.pallas_call(predictor_kernel, out_shape=(jax.ShapeDtypeStruct(((npred...  3.18 us
    pallas_call x1, Pallas kernels, local(): pl.pallas_call(send_kernel, out_shape=jax.ShapeDtypeStruct((devices, LANE...  1.47 us
  transfers between devices with their start and end apart: 1, of which 1 were waited for; matrix products, arithmetic and copies ran while one was open for 0% of the time, Pallas kernels for 5%

profile of v4, /device:TPU:1, one launch (start us, length us, event | category | flops | bytes accessed | tf_op | source)
XLA Modules:
  0.0 63.8 jit_solution(5160615294022423781)
XLA Ops:
  0.6 1.5 %send.1 = f32[128,128]{1,0:T(8,128)} custom-call(f32[8,128]{1,0:T(8,128)} %bitcast.21, s32[8,128]{1,0:T(8,128)} %bitcast.22, f32[8,128]{1,0:T(8,128)} %bitcast.23), custom_call_target="tpu_custom_call" | custom-call | tf_op jit(solution)/shard_map/send/pallas_call | solution.py:446
  2.1 11.5 %all-to-all-start = ((f32[128,1,128]{2,1,0:T(1,128)}), f32[128,1,128]{2,1,0:T(1,128)S(1)}, u32[]{:S(2)}, u32[]{:S(2)}) async-start(f32[128,1,128]{2,1,0:T(1,128)} %bitcast.9), calls=%async_computation | async-start | bytes 131072 | tf_op jit(solution)/shard_map/all_to_all | solution.py:426
  13.6 3.2 %predictors.1 = (bf16[1120,1024]{1,0:T(8,128)(2,1)S(1)}, bf16[224,80]{1,0:T(8,128)(2,1)S(1)}, bf16[112,160]{1,0:T(8,128)(2,1)S(1)}, f32[6,56,128]{2,1,0:T(8,128)...) custom-call(f32[10,32,1024]{2,1,0:T(8,128)} %state_hbm.1, ...), custom_call_target="tpu_custom_call" | custom-call | tf_op jit(solution)/shard_map/predictors/pallas_call | solution.py:465
  16.8 6.3 %all-to-all-done = f32[128,1,128]{2,1,0:T(1,128)S(1)} async-done(((f32[128,1,128]{2,1,0:T(1,128)}), f32[128,1,128]{2,1,0:T(1,128)S(1)}, u32[]{:S(2)}, u32[]{:S(2)}) %all-to-all-start) | async-done | bytes 65568 | tf_op jit(solution)/shard_map/all_to_all | solution.py:426
  23.1 26.0 %physics.1 = (f32[32,1024]{1,0:T(8,128)}, f32[128,128]{1,0:T(8,128)S(1)}) custom-call(s32[1]{0:T(128)} %bitcast.shift_ref, bf16[1120,1024]{1,0:T(8,128)(2,1)S(1)} %get-tuple-element.11.pred_ref, f32[128,128]{1,0:T(8,128)S(1)} %bitcast.16, bf16[128,1024]{1,0:T(8,128)(2,1)S(1)} %get-tuple-element.12.owner_ref, s32[1,1024]{1,0:T(1,128)S(1)} %get-tuple-element.13.slot_ref, ...), custom_call_target="tpu_custom_call" | custom-call | tf_op jit(solution)/shard_map/physics/pallas_call | solution.py:498
  49.1 13.9 %all_to_all.10 = f32[128,1,128]{2,1,0:T(1,128)S(1)} all-to-all(f32[128,1,128]{2,1,0:T(1,128)S(1)} %bitcast.18), channel_id=1, replica_groups=mesh['gx'=8,'gy'=16] {'gx','gy'}, dimensions={0} | all-to-all | bytes 131072 | tf_op jit(solution)/shard_map/all_to_all | solution.py:426
  63.0 0.9 %receive.1 = f32[3,1024]{1,0:T(4,128)} custom-call(f32[128,128]{1,0:T(8,128)S(1)} %bitcast.17), custom_call_target="tpu_custom_call" | custom-call | tf_op jit(solution)/shard_map/receive/pallas_call | solution.py:536
Async XLA Ops:
  2.1 21.0 %all-to-all-start = ((f32[128,1,128]{2,1,0:T(1,128)}), f32[128,1,128]{2,1,0:T(1,128)S(1)}, u32[]{:S(2)}, u32[]{:S(2)}) async-start(f32[128,1,128]{2,1,0:T(1,128)} %bitcast.9), calls=%async_computation | async-start | bytes 131072 | tf_op jit(solution)/shard_map/all_to_all | solution.py:426
